TPU v7x, 32 devices: a whole 2x2x4 slice. The times are simulated.
32 devices in a mesh: ri: 16 (over z, y, core), rj: 2 (over x).
Axes of the slice: x: 2, y: 2, z: 4, core: 2. Of those that a mesh axis runs over, the one named last changes fastest.
Arguments:
- pair: bfloat16 [64, 512, 512], P(None, 'ri', 'rj'), may hold values from -6 to 6
- conv1_weight: bfloat16 [3, 3, 64, 64], replicated, may hold values from -0.25 to 0.25
- conv1_bias: float32 [64], replicated, may hold values from -3 to 3
- conv2_weight: bfloat16 [3, 3, 64, 64], replicated, may hold values from -0.25 to 0.25
- conv2_bias: float32 [64], replicated, may hold values from -3 to 3
- head_weight: bfloat16 [64, 37], replicated, may hold values from -60 to 60, as said below
- head_bias: float32 [37], replicated, may hold values from -4 to 4
- bins: int32 [512, 512], P('ri', 'rj'), may hold values from 0 to 36
- mask: int32 [512], replicated, may hold values from 0 to 1, as said below
Outputs:
- grad_pair: bfloat16 [64, 512, 512], P(None, 'ri', 'rj')
- grad_conv1_weight: float32 [3, 3, 64, 64], replicated
- grad_conv1_bias: float32 [64], replicated
- grad_conv2_weight: float32 [3, 3, 64, 64], replicated
- grad_conv2_bias: float32 [64], replicated
- grad_head_weight: float32 [64, 37], replicated
- grad_head_bias: float32 [37], replicated
Inputs may be any that keep to these rules, and one draw needn't show every extreme that they name: `mask`: residue 0 is always valid; all valid residues lie before some position that is at least 256. `head_weight`: some bins' weights may reach tens in magnitude, so that logits may reach hundreds.
All inputs are finite; a program needn't handle non-finite values.
Results may differ from a plain program's by a relative error of at most 0.012.
The roundings to bfloat16 on the way count: a program that leaves them out, or rounds other values in their place, can miss the bound.
Values may be sent and summed in bfloat16 or wider, within the bound.
A program may use at most 128 MiB of HBM per device.

v0:
```python
import jax
import jax.numpy as jnp
from jax import lax
from jax.sharding import PartitionSpec as P

KERNEL_TAPS = 3
DILATION_RATE = 8


def with_halo(cells, sides, width):
    for axis, dim in sides:
        count = lax.axis_size(axis)
        ends = count - 1
        head = lax.slice_in_dim(cells, 0, width, axis=dim)
        tail = lax.slice_in_dim(cells, cells.shape[dim] - width, cells.shape[dim], axis=dim)
        cells = jnp.concatenate(
            [
                lax.ppermute(tail, axis, [(i, (i + 1) % count) for i in range(ends)]),
                cells,
                lax.ppermute(head, axis, [((i + 1) % count, i) for i in range(ends)]),
            ],
            axis=dim,
        )
    return cells


def activate(value):
    return jnp.where(value > 0, value, jnp.expm1(jnp.minimum(value, 0.0)))


def activate_slope(value):
    return jnp.where(value > 0, 1.0, jnp.exp(jnp.minimum(value, 0.0)))


def with_rims(residual_block):
    return with_halo(residual_block, (("ri", 1), ("rj", 2)), DILATION_RATE * (KERNEL_TAPS // 2))


def dilated(padded_field, weight):
    return lax.conv_general_dilated(
        padded_field[None],
        weight,
        (1, 1),
        [(0, 0), (0, 0)],
        rhs_dilation=(DILATION_RATE, DILATION_RATE),
        dimension_numbers=("NCHW", "HWIO", "NCHW"),
        preferred_element_type=jnp.float32,
    )[0]


def flipped(weight):
    return jnp.transpose(weight[::-1, ::-1], (0, 1, 3, 2))


def tap_sums(padded_field, grad):
    row_extent = grad.shape[1]
    column_extent = grad.shape[2]
    tap_rows = []
    for row_stride in range(KERNEL_TAPS):
        across = []
        for column_stride in range(KERNEL_TAPS):
            sliding_window = padded_field[
                :,
                DILATION_RATE * row_stride : DILATION_RATE * row_stride + row_extent,
                DILATION_RATE * column_stride : DILATION_RATE * column_stride + column_extent,
            ]
            across.append(
                jnp.einsum("cij,dij->cd", sliding_window, grad, preferred_element_type=jnp.float32)
            )
        tap_rows.append(jnp.stack(across))
    return jnp.stack(tap_rows)


def mirror(residual_block, first_move, second_move):
    chan_count, row_count, col_count = residual_block.shape
    col_groups = lax.axis_size("rj")
    row_groups = lax.axis_size("ri") // col_groups
    depth_rows = row_count // col_groups
    sectioned = first_move(residual_block.reshape(chan_count, col_groups, depth_rows, col_count))
    sectioned = sectioned.reshape(chan_count, depth_rows, col_groups * col_count)
    arrived = second_move(sectioned)
    arrived = arrived.reshape(chan_count, row_groups, depth_rows, col_groups, row_count)
    return jnp.transpose(arrived, (0, 4, 1, 3, 2)).reshape(chan_count, row_count, col_count)


def feature_first(sectioned):
    return lax.all_to_all(sectioned, "rj", split_axis=1, concat_axis=3, tiled=True)


def feature_second(sectioned):
    return lax.all_to_all(
        lax.all_to_all(sectioned, "ri", split_axis=2, concat_axis=1, tiled=True),
        "rj",
        split_axis=1,
        concat_axis=2,
        tiled=True,
    )


def slope_first(sectioned):
    return lax.all_to_all(sectioned, "rj", split_axis=1, concat_axis=3, tiled=True)


def slope_second(sectioned):
    return lax.all_to_all(
        lax.all_to_all(sectioned, "ri", split_axis=2, concat_axis=1, tiled=True),
        "rj",
        split_axis=1,
        concat_axis=2,
        tiled=True,
    )


def on_device(
    pair, conv1_weight, conv1_bias, conv2_weight, conv2_bias, head_weight, head_bias, bins, mask
):
    row_count = pair.shape[1]
    col_count = pair.shape[2]
    row_valid = lax.dynamic_slice_in_dim(mask, lax.axis_index("ri") * row_count, row_count).astype(
        jnp.float32
    )
    col_valid = lax.dynamic_slice_in_dim(mask, lax.axis_index("rj") * col_count, col_count).astype(
        jnp.float32
    )
    pair_mask = row_valid[:, None] * col_valid[None, :]
    n_valid = jnp.sum(mask.astype(jnp.float32))
    pair_pad = with_rims(pair)
    inner = dilated(pair_pad, conv1_weight) + conv1_bias[:, None, None]
    inner_act = activate(inner).astype(jnp.bfloat16)
    act_pad = with_rims(inner_act)
    outer = dilated(act_pad, conv2_weight) + conv2_bias[:, None, None]
    summed = pair.astype(jnp.float32) + outer
    hidden = (pair_mask[None] * activate(summed)).astype(jnp.bfloat16)
    mirrored = mirror(hidden, feature_first, feature_second)
    logits = 0.5 * (
        jnp.einsum("ck,cij->kij", head_weight, hidden, preferred_element_type=jnp.float32)
        + jnp.einsum("ck,cij->kij", head_weight, mirrored, preferred_element_type=jnp.float32)
    )
    logits = logits + head_bias[:, None, None]
    peak_logit = jnp.max(logits, axis=0, keepdims=True)
    powered = jnp.exp(logits - peak_logit)
    chance = powered / jnp.sum(powered, axis=0, keepdims=True)
    bin_ids = jnp.arange(head_weight.shape[1], dtype=jnp.int32)[:, None, None]
    onehot = (bins[None, :, :] == bin_ids).astype(jnp.float32)
    error = pair_mask[None] * (chance - onehot)
    symmetric = 0.5 * (hidden.astype(jnp.float32) + mirrored.astype(jnp.float32))
    head_term = jnp.einsum(
        "cij,kij->ck",
        symmetric,
        error,
        precision=lax.Precision.HIGHEST,
        preferred_element_type=jnp.float32,
    )
    head_bias_term = jnp.sum(error, axis=(1, 2))
    weight_wide = head_weight.astype(jnp.float32)
    slope = jnp.einsum(
        "ck,kij->cij",
        weight_wide,
        error,
        precision=lax.Precision.HIGHEST,
        preferred_element_type=jnp.float32,
    )
    slope_mirrored = mirror(slope, slope_first, slope_second)
    half_slope = 0.5 * (slope + slope_mirrored)
    outer_grad = half_slope * pair_mask[None] * activate_slope(summed)
    outer_half = outer_grad.astype(jnp.bfloat16)
    conv2_term = tap_sums(act_pad, outer_half)
    conv2_bias_term = jnp.sum(outer_grad, axis=(1, 2))
    inner_grad = dilated(with_rims(outer_half), flipped(conv2_weight)) * activate_slope(inner)
    inner_half = inner_grad.astype(jnp.bfloat16)
    conv1_term = tap_sums(pair_pad, inner_half)
    conv1_bias_term = jnp.sum(inner_grad, axis=(1, 2))
    grad_pair = (outer_grad + dilated(with_rims(inner_half), flipped(conv1_weight))).astype(
        jnp.bfloat16
    )
    totals = lax.psum(
        (conv1_term, conv1_bias_term, conv2_term, conv2_bias_term, head_term, head_bias_term),
        ("ri", "rj"),
    )
    return (
        grad_pair,
        totals[0] / n_valid,
        totals[1] / n_valid,
        totals[2] / n_valid,
        totals[3] / n_valid,
        totals[4] / n_valid,
        totals[5] / n_valid,
    )


def solution(mesh):
    return jax.shard_map(
        on_device,
        mesh=mesh,
        in_specs=(P(None, "ri", "rj"), P(), P(), P(), P(), P(), P(), P("ri", "rj"), P()),
        out_specs=(P(None, "ri", "rj"), P(), P(), P(), P(), P(), P()),
        check_vma=False,
    )
```

profile of v0, /device:TPU:0, one launch (start us, length us, event | category | flops | bytes accessed | tf_op | source)
XLA Modules:
  0.0 720.5 jit_solution(4406372204763931923)
XLA Ops:
  33.1 6.0 copy.145
  58.7 5.9 collective-permute-start.4
  91.3 6.0 copy.154
  117.2 16.0 %all_to_all.96 = bf16[64,2,16,256]{3,2,0,1:T(8,128)(2,1)} all-to-all(bf16[64,2,16,256]{3,2,0,1:T(8,128)(2,1)S(1)} %copy.159), channel_id=1, replica_groups=mesh['ri'=16,'rj'=2] {'rj'}, dimensions={1} | all-to-all | bytes 2097152 | tf_op jit(solution)/shard_map/all_to_all | solution.py:87
  133.3 5.1 copy.205
  143.0 37.1 %all_to_all.97 = bf16[16,2,16384]{2,1,0:T(2,128)(2,1)} all-to-all(bf16[16,2,16384]{2,1,0:T(2,128)(2,1)} %reshape.155), channel_id=1, replica_groups=mesh['ri'=16,'rj'=2] {'ri'}, dimensions={0} | all-to-all | bytes 2097152 | tf_op jit(solution)/shard_map/all_to_all | solution.py:92
  180.1 4.7 reshape.156
  199.0 12.2 %all-to-all-done.2 = bf16[2,2,131072]{2,1,0:T(2,128)(2,1)} async-done(((bf16[2,2,131072]{2,1,0:T(2,128)(2,1)}), bf16[2,2,131072]{2,1,0:T(2,128)(2,1)}, u32[]{:S(2)}, u32[]{:S(2)}) %all-to-all-start.2) | async-done | bytes 1048608 | tf_op jit(solution)/shard_map/all_to_all | solution.py:91
  218.5 5.1 fusion.153
  227.6 29.0 %all_to_all.98 = f32[64,2,16,256]{3,2,0,1:T(8,128)} all-to-all(f32[64,2,16,256]{3,2,0,1:T(8,128)S(1)} %copy.167), channel_id=1, replica_groups=mesh['ri'=16,'rj'=2] {'rj'}, dimensions={1} | all-to-all | bytes 4194304 | tf_op jit(solution)/shard_map/all_to_all | solution.py:101
  256.6 5.3 copy.208
  261.9 5.5 reshape.159
  273.1 39.8 %all-to-all-done.4 = f32[16,1,32768]{2,1,0:T(1,128)} async-done(((f32[16,1,32768]{2,1,0:T(1,128)}), f32[16,1,32768]{2,1,0:T(1,128)}, u32[]{:S(2)}, u32[]{:S(2)}) %all-to-all-start.4) | async-done | bytes 2097184 | tf_op jit(solution)/shard_map/all_to_all | solution.py:106
  313.4 8.7 %reduce = f32[16,32768]{1,0:T(8,128)} reduce(f32[16,1,32768]{2,1,0:T(1,128)} %all-to-all-done.4, f32[]{:T(128)} %broadcast.123), dimensions={1}, to_apply=%all_to_all.83.reduce_sub_computation | reduce | bytes 4194308 | tf_op jit(solution)/shard_map/all_to_all | solution.py:106
  326.3 5.5 copy.171
  331.9 5.2 reshape.161
  337.1 4.8 all-to-all-start.5
  341.9 5.1 maximum_maximum_fusion
  352.0 4.8 fusion.91
  356.8 11.2 %all-to-all-done.5 = f32[2,1,262144]{2,1,0:T(1,128)} async-done(((f32[2,1,262144]{2,1,0:T(1,128)}), f32[2,1,262144]{2,1,0:T(1,128)}, u32[]{:S(2)}, u32[]{:S(2)}) %all-to-all-start.5) | async-done | bytes 2097184 | tf_op jit(solution)/shard_map/all_to_all | solution.py:105
  368.0 9.5 %reduce.1 = f32[2,262144]{1,0:T(2,128)} reduce(f32[2,1,262144]{2,1,0:T(1,128)} %all-to-all-done.5, f32[]{:T(128)} %broadcast.123), dimensions={1}, to_apply=%all_to_all.87.reduce_sub_computation | reduce | bytes 4194308 | tf_op jit(solution)/shard_map/all_to_all | solution.py:105
  377.5 5.9 reshape.162
  383.4 6.6 copy.173
  394.2 5.0 fusion.143
  436.5 6.0 copy.179
  446.4 5.5 broadcast_select_fusion.1
  455.8 4.7 copy.216
  474.1 5.2 collective-permute-start.12
  480.6 48.6 %all-reduce = (f32[64]{0:T(128)S(1)}, f32[64]{0:T(128)S(1)}, f32[64,37]{0,1:T(8,128)S(1)}, f32[37]{0:T(128)}) all-reduce(f32[64]{0:T(128)} %get-tuple-element.43, f32[64]{0:T(128)} %get-tuple-element.41, f32[64,37]{0,1:T(8,128)} %fusion.91, f32[37]{0:T(128)} %fusion.142), channel_id=1, replica_groups=mesh['ri'=16,'rj'=2] {'ri','rj'}, use_global_device_ids=true, to_apply=%region_5.6 | all-reduce | flops 2533 | bytes 20264 | tf_op jit(solution)/shard_map/psum | solution.py:176
  536.9 126.6 %all-reduce.4.cloned.1.call-done = (f32[3,3,64,64]{3,2,1,0:T(8,128)}, f32[3,3,64,64]{3,2,1,0:T(8,128)}) async-done(((f32[3,3,64,64]{3,2,1,0:T(8,128)}, f32[3,3,64,64]{3,2,1,0:T(8,128)}), (f32[3,3,64,64]{3,2,1,0:T(8,128)}, f32[3,3,64,64]{3,2,1,0:T(8,128)})) %all-reduce.4.cloned.1.call-update) | async-done | bytes 294928 | tf_op jit(solution)/shard_map/psum | solution.py:176
  685.2 6.0 copy.188
  695.3 5.5 broadcast_select_fusion
  (205 shorter events, 247.4 us)
Async XLA Ops:
  7.2 93.9 %copy-start = (bf16[3,3,64,64]{3,2,1,0:T(8,128)(2,1)S(1)}, bf16[3,3,64,64]{3,2,1,0:T(8,128)(2,1)}, u32[]{:S(2)}) copy-start(bf16[3,3,64,64]{3,2,1,0:T(8,128)(2,1)} %param.12) | copy-start | bytes 221188
  7.2 6.4 copy-start.4
  9.1 3.7 copy-start.10
  9.2 3.7 collective-permute-start
  11.5 5.5 collective-permute-start.1
  18.5 5.6 collective-permute-start.2
  22.2 6.6 collective-permute-start.3
  30.1 3.0 copy-start.8
  58.7 10.0 %collective-permute-start.4 = (bf16[64,8,256]{2,0,1:T(8,128)(2,1)}, bf16[64,8,256]{2,0,1:T(8,128)(2,1)}, u32[]{:S(2)}, u32[]{:S(2)}) collective-permute-start(bf16[64,8,256]{2,0,1:T(8,128)(2,1)} %get-tuple-element.59), channel_id=1, source_target_pairs={{0,2},{2,4},{4,6},{6,8},{8,10},{10,12},{12,14},{14,16},{16,18},{18... | collective-permute-start | bytes 786440 | tf_op jit(solution)/shard_map/ppermute | solution.py:18
  64.7 4.1 collective-permute-start.5
  73.6 7.0 collective-permute-start.6
  78.0 6.8 collective-permute-start.7
  116.6 16.6 %copy-start.6 = (bf16[64,32,256]{2,0,1:T(8,128)(2,1)}, bf16[64,32,256]{2,0,1:T(8,128)(2,1)S(1)}, u32[]{:S(2)}) copy-start(bf16[64,32,256]{2,0,1:T(8,128)(2,1)S(1)} %fusion.40) | copy-start | bytes 3145732
  191.9 19.3 %all-to-all-start.2 = ((bf16[2,2,131072]{2,1,0:T(2,128)(2,1)}), bf16[2,2,131072]{2,1,0:T(2,128)(2,1)}, u32[]{:S(2)}, u32[]{:S(2)}) async-start(bf16[2,2,131072]{2,1,0:T(2,128)(2,1)} %reshape.157), calls=%async_computation.2 | async-start | bytes 2097152 | tf_op jit(solution)/shard_map/all_to_all | solution.py:91
  267.4 45.5 %all-to-all-start.4 = ((f32[16,1,32768]{2,1,0:T(1,128)}), f32[16,1,32768]{2,1,0:T(1,128)}, u32[]{:S(2)}, u32[]{:S(2)}) async-start(f32[16,1,32768]{2,1,0:T(1,128)} %reshape.159), calls=%async_computation.4 | async-start | bytes 4194304 | tf_op jit(solution)/shard_map/all_to_all | solution.py:106
  337.1 31.0 %all-to-all-start.5 = ((f32[2,1,262144]{2,1,0:T(1,128)}), f32[2,1,262144]{2,1,0:T(1,128)}, u32[]{:S(2)}, u32[]{:S(2)}) async-start(f32[2,1,262144]{2,1,0:T(1,128)} %reshape.161), calls=%async_computation.5 | async-start | bytes 4194304 | tf_op jit(solution)/shard_map/all_to_all | solution.py:105
  341.9 321.6 %all-reduce.4.cloned.1.call-start = ((), (), s32[]{:S(2)}) async-start(), calls=%async_computation.6 | async-start | bytes 1179648 | tf_op jit(solution)/shard_map/psum | solution.py:176
  399.2 2.8 copy-start.13
  399.3 15.2 %copy-start.1 = (bf16[64,32,256]{2,0,1:T(8,128)(2,1)}, bf16[64,32,256]{2,0,1:T(8,128)(2,1)S(1)}, u32[]{:S(2)}) copy-start(bf16[64,32,256]{2,0,1:T(8,128)(2,1)S(1)} %convert_element_type.43) | copy-start | bytes 3145732
  406.2 7.3 %collective-permute-start.8 = (bf16[64,8,256]{2,0,1:T(8,128)(2,1)S(1)}, bf16[64,8,256]{2,0,1:T(8,128)(2,1)S(1)}, u32[]{:S(2)}, u32[]{:S(2)}) collective-permute-start(bf16[64,8,256]{2,0,1:T(8,128)(2,1)S(1)} %get-tuple-element.57), channel_id=1, source_target_pairs={{0,2},{2,4},{4,6},{6,8},{8,10},{10,12},{12,14},{14,16},{16,18},{18... | collective-permute-start | bytes 786440 | tf_op jit(solution)/shard_map/ppermute | solution.py:18
  408.0 6.5 collective-permute-start.9
  413.4 2.9 copy-start.16
  416.3 15.7 %copy-start.2 = (bf16[64,32,256]{2,0,1:T(8,128)(2,1)S(1)}, bf16[64,32,256]{2,0,1:T(8,128)(2,1)}, u32[]{:S(2)}) copy-start(bf16[64,32,256]{2,0,1:T(8,128)(2,1)} %copy-done.1) | copy-start | bytes 3145732
  418.4 7.7 %collective-permute-start.10 = (bf16[64,48,8]{0,2,1:T(8,128)(2,1)}, bf16[64,48,8]{0,2,1:T(8,128)(2,1)}, u32[]{:S(2)}, u32[]{:S(2)}) collective-permute-start(bf16[64,48,8]{0,2,1:T(8,128)(2,1)} %copy.175), channel_id=1, source_target_pairs={{0,1},{2,3},{4,5},{6,7},{8,9},{10,11},{12,13},{14,15},{16,17},{18,... | collective-permute-start | bytes 147464 | tf_op jit(solution)/shard_map/ppermute | solution.py:18
  423.1 6.8 collective-permute-start.11
  473.3 60.7 %copy-start.11 = (bf16[64,32,256]{2,0,1:T(8,128)(2,1)S(1)}, bf16[64,32,256]{2,0,1:T(8,128)(2,1)}, u32[]{:S(2)}) copy-start(bf16[64,32,256]{2,0,1:T(8,128)(2,1)} %copy-done.10) | copy-start | bytes 3145732
  473.3 60.7 %copy-start.19 = (bf16[64,8,256]{2,0,1:T(8,128)(2,1)S(1)}, bf16[64,8,256]{2,0,1:T(8,128)(2,1)}, u32[]{:S(2)}) copy-start(bf16[64,8,256]{2,0,1:T(8,128)(2,1)} %copy-done.18) | copy-start | bytes 786436
  474.1 191.8 %collective-permute-start.12 = (bf16[64,8,256]{2,0,1:T(8,128)(2,1)}, bf16[64,8,256]{2,0,1:T(8,128)(2,1)S(1)}, u32[]{:S(2)}, u32[]{:S(2)}) collective-permute-start(bf16[64,8,256]{2,0,1:T(8,128)(2,1)} %get-tuple-element.55), channel_id=1, source_target_pairs={{0,2},{2,4},{4,6},{6,8},{8,10},{10,12},{12,14},{14,16},{16,18},{18... | collective-permute-start | bytes 786440 | tf_op jit(solution)/shard_map/ppermute | solution.py:18
  479.3 186.5 %collective-permute-start.13 = (bf16[64,8,256]{2,0,1:T(8,128)(2,1)S(1)}, bf16[64,8,256]{2,0,1:T(8,128)(2,1)S(1)}, u32[]{:S(2)}, u32[]{:S(2)}) collective-permute-start(bf16[64,8,256]{2,0,1:T(8,128)(2,1)S(1)} %get-tuple-element.56), channel_id=1, source_target_pairs={{2,0},{4,2},{6,4},{8,6},{10,8},{12,10},{14,12},{16,14},{18,16},{20... | collective-permute-start | bytes 786440 | tf_op jit(solution)/shard_map/ppermute | solution.py:20
  532.3 2.1 copy-start.21
  670.1 7.2 %collective-permute-start.14 = (bf16[64,48,8]{0,2,1:T(8,128)(2,1)S(1)}, bf16[64,48,8]{0,2,1:T(8,128)(2,1)S(1)}, u32[]{:S(2)}, u32[]{:S(2)}) collective-permute-start(bf16[64,48,8]{0,2,1:T(8,128)(2,1)S(1)} %copy.184), channel_id=1, source_target_pairs={{0,1},{2,3},{4,5},{6,7},{8,9},{10,11},{12,13},{14,15},{16,17},{18,... | collective-permute-start | bytes 147464 | tf_op jit(solution)/shard_map/ppermute | solution.py:18
  673.8 6.6 collective-permute-start.15
  (19 other events, 22.9 us)
Sparse Core Ops, SparseCore 0:
  535.4 128.1 all-reduce.3
where the time goes:
time: 726 us; the launch traced here: 720 us
  waiting for transfers between devices  205 us (28%)
  local copies, waits for them, and re-layouts  188 us (26%)
  blocking collectives  131 us (18%)
  other arithmetic  78.8 us (11%)
  starting transfers between devices  51.9 us (7%)
  matrix products  51.3 us (7%)
  between operations  15 us (2%)
    psum x1, waiting for transfers between devices, on_device(): lax.psum((conv1_term, conv1_bias_term, conv2_term, conv2_bias_term, head_...  127 us
    unnamed x78, local copies, waits for them, and re-layouts  67.4 us
    psum x1, blocking collectives, on_device(): lax.psum((conv1_term, conv1_bias_term, conv2_term, conv2_bias_term, head_...  48.6 us
    all_to_all x1, waiting for transfers between devices, slope_second(): lax.all_to_all(sectioned, 'ri', split_axis=2, concat_axis=1, tiled=True)  39.8 us
    all_to_all x1, blocking collectives, feature_second(): lax.all_to_all(sectioned, 'ri', split_axis=2, concat_axis=1, tiled=True)  37.1 us
    conv_general_dilated x16, local copies, waits for them, and re-layouts, dilated(): lax.conv_general_dilated(padded_field[None], weight, (1, 1), [(0, 0), (0,...  30.2 us
    all_to_all x1, blocking collectives, slope_first(): lax.all_to_all(sectioned, 'rj', split_axis=1, concat_axis=3, tiled=True)  29 us
    ppermute x8, starting transfers between devices, with_halo(): lax.ppermute(tail, axis, [(i, (i + 1) % count) for i in range(ends)])  27.1 us
  transfers between devices with their start and end apart: 20, of which 11 were waited for; matrix products, arithmetic and copies ran while one was open for 7% of the time, Pallas kernels for 0%

commit v1 on v0

--- a/solution.py
+++ b/solution.py
@@ -1,6 +1,10 @@
+import functools
+
 import jax
 import jax.numpy as jnp
 from jax import lax
+from jax.experimental import pallas as pl
+from jax.experimental.pallas import tpu as pltpu
 from jax.sharding import PartitionSpec as P
 
 KERNEL_TAPS = 3
@@ -71,44 +75,123 @@
     return jnp.stack(tap_rows)
 
 
-def mirror(residual_block, first_move, second_move):
-    chan_count, row_count, col_count = residual_block.shape
-    col_groups = lax.axis_size("rj")
-    row_groups = lax.axis_size("ri") // col_groups
-    depth_rows = row_count // col_groups
-    sectioned = first_move(residual_block.reshape(chan_count, col_groups, depth_rows, col_count))
-    sectioned = sectioned.reshape(chan_count, depth_rows, col_groups * col_count)
-    arrived = second_move(sectioned)
-    arrived = arrived.reshape(chan_count, row_groups, depth_rows, col_groups, row_count)
-    return jnp.transpose(arrived, (0, 4, 1, 3, 2)).reshape(chan_count, row_count, col_count)
-
-
-def feature_first(sectioned):
-    return lax.all_to_all(sectioned, "rj", split_axis=1, concat_axis=3, tiled=True)
-
-
-def feature_second(sectioned):
-    return lax.all_to_all(
-        lax.all_to_all(sectioned, "ri", split_axis=2, concat_axis=1, tiled=True),
-        "rj",
-        split_axis=1,
-        concat_axis=2,
-        tiled=True,
-    )
-
-
-def slope_first(sectioned):
-    return lax.all_to_all(sectioned, "rj", split_axis=1, concat_axis=3, tiled=True)
-
-
-def slope_second(sectioned):
-    return lax.all_to_all(
-        lax.all_to_all(sectioned, "ri", split_axis=2, concat_axis=1, tiled=True),
-        "rj",
-        split_axis=1,
-        concat_axis=2,
-        tiled=True,
-    )
+def swap_kernel(count, src, dst, send_sem, recv_sem, own_sem):
+    row = lax.axis_index("ri")
+    column = lax.axis_index("rj")
+    slot = lax.rem(row, count)
+    far_column = lax.div(row, count)
+    own_group = far_column == column
+    barrier = pltpu.get_barrier_semaphore()
+
+    def meets_self(block):
+        return jnp.logical_and(own_group, slot == block)
+
+    def exchange(block):
+        return pltpu.make_async_remote_copy(
+            src_ref=src.at[block],
+            dst_ref=dst.at[slot],
+            send_sem=send_sem.at[block],
+            recv_sem=recv_sem.at[slot],
+            device_id=(count * column + block, far_column),
+            device_id_type=pl.DeviceIdType.MESH,
+        )
+
+    def arrival(block):
+        return pltpu.make_async_remote_copy(
+            src_ref=src.at[block],
+            dst_ref=dst.at[block],
+            send_sem=send_sem.at[block],
+            recv_sem=recv_sem.at[block],
+            device_id=(count * column + block, far_column),
+            device_id_type=pl.DeviceIdType.MESH,
+        )
+
+    for block in range(count):
+
+        @pl.when(jnp.logical_not(meets_self(block)))
+        def _():
+            pl.semaphore_signal(
+                barrier,
+                inc=1,
+                device_id=(count * column + block, far_column),
+                device_id_type=pl.DeviceIdType.MESH,
+            )
+
+    @pl.when(own_group)
+    def _():
+        pl.semaphore_wait(barrier, count - 1)
+
+    @pl.when(jnp.logical_not(own_group))
+    def _():
+        pl.semaphore_wait(barrier, count)
+
+    for block in range(count):
+
+        @pl.when(jnp.logical_not(meets_self(block)))
+        def _():
+            exchange(block).start()
+
+        @pl.when(meets_self(block))
+        def _():
+            pltpu.make_async_copy(src.at[block], dst.at[block], own_sem).start()
+
+    for block in range(count):
+
+        @pl.when(jnp.logical_not(meets_self(block)))
+        def _():
+            arrival(block).wait()
+
+        @pl.when(meets_self(block))
+        def _():
+            pltpu.make_async_copy(src.at[block], dst.at[block], own_sem).wait()
+
+
+def swapped(blocks):
+    count = blocks.shape[0]
+    return pl.pallas_call(
+        functools.partial(swap_kernel, count),
+        out_shape=jax.ShapeDtypeStruct(blocks.shape, blocks.dtype),
+        in_specs=[pl.BlockSpec(memory_space=pl.ANY)],
+        out_specs=pl.BlockSpec(memory_space=pl.ANY),
+        scratch_shapes=[
+            pltpu.SemaphoreType.DMA((count,)),
+            pltpu.SemaphoreType.DMA((count,)),
+            pltpu.SemaphoreType.DMA,
+        ],
+        compiler_params=pltpu.CompilerParams(collective_id=0, has_side_effects=True),
+    )(blocks)
+
+
+def mirror(block):
+    chan_count, row_count, col_count = block.shape
+    count = col_count // row_count
+    parts = block.reshape(chan_count, row_count, count, row_count)
+    parts = jnp.transpose(parts, (2, 0, 3, 1)).reshape(count, -1, 128)
+    arrived = swapped(parts).reshape(count, chan_count, row_count, row_count)
+    return jnp.transpose(arrived, (1, 2, 0, 3)).reshape(chan_count, row_count, col_count)
+
+
+def summed_over_mesh(flat):
+    for axis in ("ri", "rj"):
+        size = lax.axis_size(axis)
+        stride = 1
+        while stride < size:
+            flat = flat + lax.ppermute(flat, axis, [(i, i ^ stride) for i in range(size)])
+            stride *= 2
+    return flat
+
+
+def sum_arrays(arrays):
+    flat = jnp.concatenate([a.reshape(-1) for a in arrays])
+    used = flat.shape[0]
+    flat = jnp.pad(flat, (0, -used % 1024)).reshape(-1, 128)
+    flat = summed_over_mesh(flat).reshape(-1)
+    outs = []
+    start = 0
+    for a in arrays:
+        outs.append(flat[start : start + a.size].reshape(a.shape))
+        start += a.size
+    return outs
 
 
 def on_device(
@@ -131,7 +214,10 @@
     outer = dilated(act_pad, conv2_weight) + conv2_bias[:, None, None]
     summed = pair.astype(jnp.float32) + outer
     hidden = (pair_mask[None] * activate(summed)).astype(jnp.bfloat16)
-    mirrored = mirror(hidden, feature_first, feature_second)
+    bins_field = bins.astype(jnp.bfloat16)[None]
+    swapped_all = mirror(jnp.concatenate([hidden, bins_field], axis=0))
+    mirrored = swapped_all[:-1]
+    bins_mirrored = swapped_all[-1].astype(jnp.int32)
     logits = 0.5 * (
         jnp.einsum("ck,cij->kij", head_weight, hidden, preferred_element_type=jnp.float32)
         + jnp.einsum("ck,cij->kij", head_weight, mirrored, preferred_element_type=jnp.float32)
@@ -141,27 +227,24 @@
     powered = jnp.exp(logits - peak_logit)
     chance = powered / jnp.sum(powered, axis=0, keepdims=True)
     bin_ids = jnp.arange(head_weight.shape[1], dtype=jnp.int32)[:, None, None]
-    onehot = (bins[None, :, :] == bin_ids).astype(jnp.float32)
-    error = pair_mask[None] * (chance - onehot)
-    symmetric = 0.5 * (hidden.astype(jnp.float32) + mirrored.astype(jnp.float32))
+    onehot = (bins[None] == bin_ids).astype(jnp.float32)
+    onehot_mirrored = (bins_mirrored[None] == bin_ids).astype(jnp.float32)
+    even_error = pair_mask[None] * (chance - 0.5 * (onehot + onehot_mirrored))
     head_term = jnp.einsum(
         "cij,kij->ck",
-        symmetric,
-        error,
+        hidden.astype(jnp.float32),
+        even_error,
         precision=lax.Precision.HIGHEST,
         preferred_element_type=jnp.float32,
     )
-    head_bias_term = jnp.sum(error, axis=(1, 2))
-    weight_wide = head_weight.astype(jnp.float32)
-    slope = jnp.einsum(
+    head_bias_term = jnp.sum(even_error, axis=(1, 2))
+    half_slope = jnp.einsum(
         "ck,kij->cij",
-        weight_wide,
-        error,
+        head_weight.astype(jnp.float32),
+        even_error,
         precision=lax.Precision.HIGHEST,
         preferred_element_type=jnp.float32,
     )
-    slope_mirrored = mirror(slope, slope_first, slope_second)
-    half_slope = 0.5 * (slope + slope_mirrored)
     outer_grad = half_slope * pair_mask[None] * activate_slope(summed)
     outer_half = outer_grad.astype(jnp.bfloat16)
     conv2_term = tap_sums(act_pad, outer_half)
@@ -173,18 +256,16 @@
     grad_pair = (outer_grad + dilated(with_rims(inner_half), flipped(conv1_weight))).astype(
         jnp.bfloat16
     )
-    totals = lax.psum(
-        (conv1_term, conv1_bias_term, conv2_term, conv2_bias_term, head_term, head_bias_term),
-        ("ri", "rj"),
-    )
+    late = sum_arrays((conv1_term, conv1_bias_term))
+    early = sum_arrays((conv2_term, conv2_bias_term, head_term, head_bias_term))
     return (
         grad_pair,
-        totals[0] / n_valid,
-        totals[1] / n_valid,
-        totals[2] / n_valid,
-        totals[3] / n_valid,
-        totals[4] / n_valid,
-        totals[5] / n_valid,
+        late[0] / n_valid,
+        late[1] / n_valid,
+        early[0] / n_valid,
+        early[1] / n_valid,
+        early[2] / n_valid,
+        early[3] / n_valid,
     )
 
 

time: 726 us -> 481 us (0.66)
  waiting for transfers between devices: 205 us -> 23.1 us
  blocking collectives: 131 us -> 0 us
  matrix products: 51.3 us -> 104 us
  starting transfers between devices: 51.9 us -> 80.6 us
  Pallas kernels: 0 us -> 22.5 us
  local copies, waits for them, and re-layouts: 188 us -> 171 us
  between operations: 15 us -> 1.86 us
  other arithmetic: 78.8 us -> 70.8 us
    psum x1 -> x0, waiting for transfers between devices: 127 us -> none  [on_device(): lax.psum((conv1_term, conv1_bias_term, conv2_term, conv2_bias_term, head_...]
    all_to_all x3 -> x0, blocking collectives: 82.1 us -> none  [the longest x1 37.1 us: feature_second(): lax.all_to_all(sectioned, 'ri', split_axis=2, concat_axis=1, tiled=True)]
    all_to_all x3 -> x0, waiting for transfers between devices: 63.2 us -> none  [the longest x1 39.8 us: slope_second(): lax.all_to_all(sectioned, 'ri', split_axis=2, concat_axis=1, tiled=True)]
    unnamed x78 -> x92, local copies, waits for them, and re-layouts: 67.4 us -> 15.4 us
    psum x1 -> x0, blocking collectives: 48.6 us -> none  [on_device(): lax.psum((conv1_term, conv1_bias_term, conv2_term, conv2_bias_term, head_...]
    conv_general_dilated x4, matrix products: 18.6 us -> 54.9 us  [dilated(): lax.conv_general_dilated(padded_field[None], weight, (1, 1), [(0, 0), (0,...]
    broadcast_in_dim x0 -> x2, local copies, waits for them, and re-layouts: none -> 31.3 us  [dilated(): padded_field[None]]
    ppermute x0 -> x10, starting transfers between devices: none -> 24.7 us  [summed_over_mesh(): lax.ppermute(flat, axis, [(i, i ^ stride) for i in range(size)])]
  transfers between devices with their start and end apart: 20 -> 26, of which waited for: 11 -> 8; matrix products, arithmetic and copies ran while one was open for 7% -> 29% of each run, Pallas kernels for 0% -> 0%
where the time goes in v1:
time: 481 us; the launch traced here: 474 us
  local copies, waits for them, and re-layouts  171 us (36%)
  matrix products  104 us (22%)
  starting transfers between devices  80.6 us (17%)
  other arithmetic  70.8 us (15%)
  waiting for transfers between devices  23.1 us (5%)
  Pallas kernels  22.5 us (5%)
    conv_general_dilated x4, matrix products, dilated(): lax.conv_general_dilated(padded_field[None], weight, (1, 1), [(0, 0), (0,...  54.9 us
    ppermute x8, starting transfers between devices, with_halo(): lax.ppermute(tail, axis, [(i, (i + 1) % count) for i in range(ends)])  45.5 us
    dot_general x18, matrix products, tap_sums(): jnp.einsum('cij,dij->cd', sliding_window, grad, preferred_element_type=jn...  33.1 us
    broadcast_in_dim x2, local copies, waits for them, and re-layouts, dilated(): padded_field[None]  31.3 us
    conv_general_dilated x10, local copies, waits for them, and re-layouts, dilated(): lax.conv_general_dilated(padded_field[None], weight, (1, 1), [(0, 0), (0,...  28.6 us
    ppermute x10, starting transfers between devices, summed_over_mesh(): lax.ppermute(flat, axis, [(i, i ^ stride) for i in range(size)])  24.7 us
    pallas_call x1, Pallas kernels, swapped(): pl.pallas_call(functools.partial(swap_kernel, count), out_shape=jax.Shape...  22.5 us
    concatenate x7, other arithmetic, with_halo(): jnp.concatenate([lax.ppermute(tail, axis, [(i, (i + 1) % count) for i in...  16.6 us
  transfers between devices with their start and end apart: 26, of which 8 were waited for; matrix products, arithmetic and copies ran while one was open for 29% of the time, Pallas kernels for 0%

profile of v1, /device:TPU:0, one launch (start us, length us, event | category | flops | bytes accessed | tf_op | source)
XLA Modules:
  0.0 473.6 jit_solution(8147725905266763488)
XLA Ops:
  18.0 4.3 collective-permute-done.3
  26.6 16.1 %copy.401 = bf16[1,64,48,272]{1,0,3,2:T(2,128)(2,1)} copy(bf16[1,64,48,272]{3,1,2,0:T(8,128)(2,1)} %maximum_bitcast_fusion) | data formatting | bytes 3342336 | tf_op jit(solution)/shard_map/broadcast_in_dim | solution.py:45
  42.8 21.9 %fusion.127 = f32[1,64,32,256]{1,0,3,2:T(1,128)} fusion(bf16[1,64,48,272]{1,0,3,2:T(2,128)(2,1)} %copy.401, bf16[3,3,64,64]{3,2,1,0:T(8,128)(2,1)S(1)} %copy-done.39), kind=kOutput, calls=%fused_computation.189 | convolution fusion | flops 603979776 | bytes 3842048 | tf_op jit(solution)/shard_map/conv_general_dilated | solution.py:44
  64.7 6.7 %copy.402 = f32[1,64,32,256]{3,2,1,0:T(8,128)} copy(f32[1,64,32,256]{1,0,3,2:T(1,128)} %fusion.127) | data formatting | bytes 4194304 | tf_op jit(solution)/shard_map/conv_general_dilated | solution.py:44
  74.8 5.9 %collective-permute-start.4 = (bf16[64,8,256]{2,1,0:T(8,128)(2,1)}, bf16[64,8,256]{2,1,0:T(8,128)(2,1)}, u32[]{:S(2)}, u32[]{:S(2)}) collective-permute-start(bf16[64,8,256]{2,1,0:T(8,128)(2,1)} %get-tuple-element.82), channel_id=1, source_target_pairs={{0,2},{2,4},{4,6},{6,8},{8,10},{10,12},{12,14},{14,16},{16,18},{18... | collective-permute-start | bytes 786440 | tf_op jit(solution)/shard_map/ppermute | solution.py:22
  83.9 6.0 %concatenate.93 = bf16[1,32,8,32]{0,3,2,1:T(8,128)(2,1)} reshape(bf16[32,256]{1,0:T(8,128)(2,1)} %convert_element_type.57) | data formatting | bytes 32768 | tf_op jit(solution)/shard_map/concatenate | solution.py:218
  111.0 4.3 maximum_bitcast_fusion.1
  115.4 15.1 %copy.407 = bf16[1,64,48,272]{1,0,3,2:T(2,128)(2,1)} copy(bf16[1,64,48,272]{3,2,1,0:T(8,128)(2,1)} %maximum_bitcast_fusion.1) | data formatting | bytes 3342336 | tf_op jit(solution)/shard_map/broadcast_in_dim | solution.py:45
  130.5 21.9 %fusion.128 = f32[1,64,32,256]{1,0,3,2:T(1,128)} fusion(bf16[1,64,48,272]{1,0,3,2:T(2,128)(2,1)} %copy.407, bf16[3,3,64,64]{3,2,1,0:T(8,128)(2,1)S(1)} %copy-done), kind=kOutput, calls=%fused_computation.190 | convolution fusion | flops 603979776 | bytes 3842048 | tf_op jit(solution)/shard_map/conv_general_dilated | solution.py:44
  152.4 6.8 %copy.408 = f32[1,64,32,256]{3,2,1,0:T(8,128)} copy(f32[1,64,32,256]{1,0,3,2:T(1,128)} %fusion.128) | data formatting | bytes 4194304 | tf_op jit(solution)/shard_map/conv_general_dilated | solution.py:44
  166.5 4.8 %maximum_bitcast_fusion.2 = bf16[8,65,32,32]{1,2,0,3:T(8,128)(2,1)} fusion(bf16[1,32,8,32]{0,3,2,1:T(8,128)(2,1)} %concatenate.93, bf16[64,32,8,32]{0,3,2,1:T(8,128)(2,1)} %bitcast.174), kind=kLoop, calls=%fused_computation.43 | loop fusion | flops 2129920 | bytes 2129920 | tf_op jit(solution)/shard_map/transpose | solution.py:169
  171.3 7.7 %copy.412 = bf16[8,65,32,32]{3,2,1,0:T(8,128)(2,1)} copy(bf16[8,65,32,32]{1,2,0,3:T(8,128)(2,1)} %maximum_bitcast_fusion.2) | data formatting | bytes 2129920 | tf_op jit(solution)/shard_map/transpose | solution.py:169
  179.0 6.1 %reshape.102.src = bf16[8,520,128]{2,1,0:T(8,128)(2,1)} reshape(bf16[8,65,32,32]{3,2,1,0:T(8,128)(2,1)} %copy.412) | data formatting | bytes 2129920 | tf_op jit(solution)/shard_map/reshape | solution.py:169
  185.1 22.5 %shard_map.144 = bf16[8,520,128]{2,1,0:T(8,128)(2,1)} custom-call(bf16[8,520,128]{2,1,0:T(8,128)(2,1)} %reshape.102.src), custom_call_target="tpu_custom_call" | custom-call | tf_op jit(solution)/shard_map/pallas_call | solution.py:151
  207.6 5.8 %reshape.103 = bf16[8,65,32,32]{3,2,1,0:T(8,128)(2,1)} reshape(bf16[8,520,128]{2,1,0:T(8,128)(2,1)} %shard_map.144) | data formatting | bytes 2129920 | tf_op jit(solution)/shard_map/reshape | solution.py:170
  213.4 4.9 %slice.195 = bf16[64,32,8,32]{3,1,0,2:T(8,128)(2,1)} slice(bf16[65,32,8,32]{3,1,0,2:T(8,128)(2,1)} %bitcast.175), slice={[0:64], [0:32], [0:8], [0:32]} | slice | bytes 2097152 | tf_op jit(solution)/shard_map/slice | solution.py:219
  219.8 5.7 %copy.413 = bf16[64,32,8,32]{0,3,2,1:T(8,128)(2,1)} copy(bf16[64,32,8,32]{3,1,0,2:T(8,128)(2,1)} %slice.195) | data formatting | bytes 2097152 | tf_op jit(solution)/shard_map/slice | solution.py:219
  231.9 5.1 %fusion.124 = (f32[32,256]{1,0:T(8,128)}, f32[37,32,256]{2,0,1:T(8,128)}) fusion(f32[32,256,37]{1,2,0:T(8,128)} %fusion.90, bf16[64,32,256]{0,2,1:T(8,128)(2,1)} %bitcast.181, f32[37]{0:T(128)} %param.15, bf16[64,37]{0,1:T(8,128)(2,1)} %param.14), kind=kOutput, calls=%fused_computation.188 | convolution fusion | flops 40312868 | bytes 3511060 | tf_op jit(solution)/shard_map/sub | solution.py:227
  239.6 4.9 %convolution_bitcast_fusion = f32[64,37]{1,0:T(8,128)} fusion(bf16[64,32,256]{0,2,1:T(8,128)(2,1)} %copy.410, f32[37,32,256]{2,0,1:T(8,128)} %get-tuple-element.87, s32[32,256]{1,0:T(8,128)} %reshape.125, s32[32,256]{1,0:T(8,128)} %param.16, f32[32,256]{1,0:T(8,128)} %get-tuple-element.86, f32[32,256]{1,0:T(8,128)} %broadcast_multiply_fusion), kind=kOutput, calls=%fused_computation.70 | convolution fusion | flops 235511808 | bytes 2401536 | tf_op jit(solution)/shard_map/cij,kij->ck/dot_general | solution.py:233
  276.2 5.7 %collective-permute-start.8 = (bf16[64,8,256]{2,1,0:T(8,128)(2,1)}, bf16[64,8,256]{2,1,0:T(8,128)(2,1)}, u32[]{:S(2)}, u32[]{:S(2)}) collective-permute-start(bf16[64,8,256]{2,1,0:T(8,128)(2,1)} %get-tuple-element.80), channel_id=1, source_target_pairs={{0,2},{2,4},{4,6},{6,8},{8,10},{10,12},{12,14},{14,16},{16,18},{18... | collective-permute-start | bytes 786440 | tf_op jit(solution)/shard_map/ppermute | solution.py:22
  302.0 17.5 %collective-permute-start.10 = (bf16[64,48,8]{0,2,1:T(8,128)(2,1)}, bf16[64,48,8]{0,2,1:T(8,128)(2,1)}, u32[]{:S(2)}, u32[]{:S(2)}) collective-permute-start(bf16[64,48,8]{0,2,1:T(8,128)(2,1)} %copy.417), channel_id=1, source_target_pairs={{0,1},{2,3},{4,5},{6,7},{8,9},{10,11},{12,13},{14,15},{16,17},{18,... | collective-permute-start | bytes 147464 | tf_op jit(solution)/shard_map/ppermute | solution.py:22
  324.8 12.2 %collective-permute-start.22 = (f32[312,128]{1,0:T(8,128)}, f32[312,128]{1,0:T(8,128)}, u32[]{:S(2)}, u32[]{:S(2)}) collective-permute-start(f32[312,128]{1,0:T(8,128)} %fusion.106), channel_id=1, source_target_pairs={{0,4},{2,6},{4,0},{6,2},{8,12},{10,14},{12,8},{14,10},{16,20},{18,... | collective-permute-start | bytes 479240 | tf_op jit(solution)/shard_map/ppermute | solution.py:179
  341.7 4.7 %pad_maximum_fusion = bf16[64,48,272]{2,1,0:T(8,128)(2,1)} fusion(bf16[64,48,8]{2,1,0:T(8,128)(2,1)} %copy.420, bf16[64,8,256]{2,1,0:T(8,128)(2,1)} %collective-permute-done.9, bf16[64,32,256]{2,1,0:T(8,128)(2,1)S(1)} %copy-done.7, bf16[64,8,256]{2,1,0:T(8,128)(2,1)} %collective-permute-done.8, bf16[64,48,8]{2,1,0:T(8,128)(2,1)} %copy.419), kind=kLoop, calls=%fused_computation.32 | loop fusion | flops 8355840 | bytes 3342336 | tf_op jit(solution)/shard_map/concatenate | solution.py:20
  346.4 6.5 %copy.421 = bf16[64,48,272]{0,1,2:T(8,128)(2,1)} copy(bf16[64,48,272]{2,1,0:T(8,128)(2,1)} %pad_maximum_fusion) | data formatting | bytes 3342336 | tf_op jit(solution)/shard_map/concatenate | solution.py:20
  356.8 5.5 %broadcast_select_fusion.1 = f32[32,8,34,64]{3,1,2,0:T(8,128)S(1)} fusion(pred[8,34]{0,1:T(8,128)(4,1)S(1)} %copy-done.41, bf16[3,3,64,64]{3,2,1,0:T(8,128)(2,1)S(1)} %copy-done, bf16[64,48,1,7,16]{0,3,4,1,2:T(8,128)(2,1)S(1)} %slice.201, bf16[64,48,1,8,34]{0,3,4,1,2:T(8,128)(2,1)S(1)} %copy.423), kind=kOutput, calls=%fused_computation.37 | convolution fusion | flops 649658368 | bytes 4661520 | tf_op jit(solution)/shard_map/conv_general_dilated | solution.py:44
  366.2 5.3 %copy.480 = f32[32,1,256,64]{2,0,3,1:T(8,128)} copy(f32[32,1,256,64]{3,0,2,1:T(8,128)} %slice.202) | data formatting | bytes 4194304
  393.2 5.7 %collective-permute-start.23 = (f32[312,128]{1,0:T(8,128)S(1)}, f32[312,128]{1,0:T(8,128)S(1)}, u32[]{:S(2)}, u32[]{:S(2)}) collective-permute-start(f32[312,128]{1,0:T(8,128)S(1)} %fusion.138), channel_id=1, source_target_pairs={{0,8},{2,10},{4,12},{6,14},{8,0},{10,2},{12,4},{14,6},{16,24},{18,... | collective-permute-start | bytes 479240 | tf_op jit(solution)/shard_map/ppermute | solution.py:179
  399.7 4.7 collective-permute-done.23
  409.7 5.8 %collective-permute-start.14 = (bf16[64,48,8]{0,2,1:T(8,128)(2,1)S(1)}, bf16[64,48,8]{0,2,1:T(8,128)(2,1)S(1)}, u32[]{:S(2)}, u32[]{:S(2)}) collective-permute-start(bf16[64,48,8]{0,2,1:T(8,128)(2,1)S(1)} %copy.426), channel_id=1, source_target_pairs={{0,1},{2,3},{4,5},{6,7},{8,9},{10,11},{12,13},{14,15},{16,17},{18,... | collective-permute-start | bytes 147464 | tf_op jit(solution)/shard_map/ppermute | solution.py:22
  426.8 6.5 %copy.430 = bf16[64,48,272]{0,1,2:T(8,128)(2,1)} copy(bf16[64,48,272]{2,1,0:T(8,128)(2,1)} %pad_maximum_fusion.1) | data formatting | bytes 3342336 | tf_op jit(solution)/shard_map/concatenate | solution.py:20
  437.4 5.5 %broadcast_select_fusion = f32[32,8,34,64]{3,1,2,0:T(8,128)S(1)} fusion(pred[8,34]{0,1:T(8,128)(4,1)S(1)} %copy-done.42, bf16[3,3,64,64]{3,2,1,0:T(8,128)(2,1)S(1)} %copy-done.40, bf16[64,48,1,7,16]{0,3,4,1,2:T(8,128)(2,1)S(1)} %slice.207, bf16[64,48,1,8,34]{0,3,4,1,2:T(8,128)(2,1)S(1)} %copy.432), kind=kOutput, calls=%fused_computation.36 | convolution fusion | flops 649658368 | bytes 4661520 | tf_op jit(solution)/shard_map/conv_general_dilated | solution.py:44
  446.8 5.2 %copy.481 = f32[32,1,256,64]{2,0,3,1:T(8,128)} copy(f32[32,1,256,64]{3,0,2,1:T(8,128)} %slice.208) | data formatting | bytes 4194304
  (243 shorter events, 204.4 us)
Async XLA Ops:
  0.6 129.9 %copy-start = (bf16[3,3,64,64]{3,2,1,0:T(8,128)(2,1)S(1)}, bf16[3,3,64,64]{3,2,1,0:T(8,128)(2,1)}, u32[]{:S(2)}) copy-start(bf16[3,3,64,64]{3,2,1,0:T(8,128)(2,1)} %param.12) | copy-start | bytes 221188
  2.6 4.4 collective-permute-start
  5.0 5.5 %collective-permute-start.1 = (bf16[64,8,256]{2,0,1:T(8,128)(2,1)S(1)}, bf16[64,8,256]{2,0,1:T(8,128)(2,1)S(1)}, u32[]{:S(2)}, u32[]{:S(2)}) collective-permute-start(bf16[64,8,256]{2,0,1:T(8,128)(2,1)S(1)} %get-tuple-element.84), channel_id=1, source_target_pairs={{2,0},{4,2},{6,4},{8,6},{10,8},{12,10},{14,12},{16,14},{18,16},{20... | collective-permute-start | bytes 786440 | tf_op jit(solution)/shard_map/ppermute | solution.py:24
  12.0 5.6 %collective-permute-start.2 = (bf16[64,48,8]{0,2,1:T(8,128)(2,1)S(1)}, bf16[64,48,8]{0,2,1:T(8,128)(2,1)S(1)}, u32[]{:S(2)}, u32[]{:S(2)}) collective-permute-start(bf16[64,48,8]{0,2,1:T(8,128)(2,1)S(1)} %copy.396), channel_id=1, source_target_pairs={{0,1},{2,3},{4,5},{6,7},{8,9},{10,11},{12,13},{14,15},{16,17},{18,... | collective-permute-start | bytes 147464 | tf_op jit(solution)/shard_map/ppermute | solution.py:22
  15.7 6.6 %collective-permute-start.3 = (bf16[64,48,8]{0,2,1:T(8,128)(2,1)S(1)}, bf16[64,48,8]{0,2,1:T(8,128)(2,1)}, u32[]{:S(2)}, u32[]{:S(2)}) collective-permute-start(bf16[64,48,8]{0,2,1:T(8,128)(2,1)S(1)} %copy.397), channel_id=1, source_target_pairs={{1,0},{3,2},{5,4},{7,6},{9,8},{11,10},{13,12},{15,14},{17,16},{19,... | collective-permute-start | bytes 147464 | tf_op jit(solution)/shard_map/ppermute | solution.py:24
  26.6 16.2 %copy-start.39 = (bf16[3,3,64,64]{3,2,1,0:T(8,128)(2,1)S(1)}, bf16[3,3,64,64]{3,2,1,0:T(8,128)(2,1)}, u32[]{:S(2)}) copy-start(bf16[3,3,64,64]{3,2,1,0:T(8,128)(2,1)} %param.10) | copy-start | bytes 221188
  71.4 11.9 %copy-start.32 = (s32[32,256]{1,0:T(8,128)S(1)}, s32[32,256]{1,0:T(8,128)}, u32[]{:S(2)}) copy-start(s32[32,256]{1,0:T(8,128)} %param.16) | copy-start | bytes 98308
  74.8 16.5 %collective-permute-start.4 = (bf16[64,8,256]{2,1,0:T(8,128)(2,1)}, bf16[64,8,256]{2,1,0:T(8,128)(2,1)}, u32[]{:S(2)}, u32[]{:S(2)}) collective-permute-start(bf16[64,8,256]{2,1,0:T(8,128)(2,1)} %get-tuple-element.82), channel_id=1, source_target_pairs={{0,2},{2,4},{4,6},{6,8},{8,10},{10,12},{12,14},{14,16},{16,18},{18... | collective-permute-start | bytes 786440 | tf_op jit(solution)/shard_map/ppermute | solution.py:22
  80.7 10.5 %collective-permute-start.5 = (bf16[64,8,256]{2,1,0:T(8,128)(2,1)}, bf16[64,8,256]{2,1,0:T(8,128)(2,1)}, u32[]{:S(2)}, u32[]{:S(2)}) collective-permute-start(bf16[64,8,256]{2,1,0:T(8,128)(2,1)} %get-tuple-element.83), channel_id=1, source_target_pairs={{2,0},{4,2},{6,4},{8,6},{10,8},{12,10},{14,12},{16,14},{18,16},{20... | collective-permute-start | bytes 786440 | tf_op jit(solution)/shard_map/ppermute | solution.py:24
  96.2 8.7 %collective-permute-start.6 = (bf16[64,48,8]{0,2,1:T(8,128)(2,1)}, bf16[64,48,8]{0,2,1:T(8,128)(2,1)}, u32[]{:S(2)}, u32[]{:S(2)}) collective-permute-start(bf16[64,48,8]{0,2,1:T(8,128)(2,1)} %copy.403), channel_id=1, source_target_pairs={{0,1},{2,3},{4,5},{6,7},{8,9},{10,11},{12,13},{14,15},{16,17},{18,... | collective-permute-start | bytes 147464 | tf_op jit(solution)/shard_map/ppermute | solution.py:22
  101.0 7.7 %collective-permute-start.7 = (bf16[64,48,8]{0,2,1:T(8,128)(2,1)}, bf16[64,48,8]{0,2,1:T(8,128)(2,1)}, u32[]{:S(2)}, u32[]{:S(2)}) collective-permute-start(bf16[64,48,8]{0,2,1:T(8,128)(2,1)} %copy.404), channel_id=1, source_target_pairs={{1,0},{3,2},{5,4},{7,6},{9,8},{11,10},{13,12},{15,14},{17,16},{19,... | collective-permute-start | bytes 147464 | tf_op jit(solution)/shard_map/ppermute | solution.py:24
  249.1 24.8 %copy-start.6 = (bf16[64,32,256]{2,1,0:T(8,128)(2,1)}, bf16[64,32,256]{2,1,0:T(8,128)(2,1)S(1)}, u32[]{:S(2)}) copy-start(bf16[64,32,256]{2,1,0:T(8,128)(2,1)S(1)} %convert_element_type.62) | copy-start | bytes 3145732
  276.2 20.8 %copy-start.7 = (bf16[64,32,256]{2,1,0:T(8,128)(2,1)S(1)}, bf16[64,32,256]{2,1,0:T(8,128)(2,1)}, u32[]{:S(2)}) copy-start(bf16[64,32,256]{2,1,0:T(8,128)(2,1)} %copy-done.6) | copy-start | bytes 3145732
  276.2 20.7 %collective-permute-start.8 = (bf16[64,8,256]{2,1,0:T(8,128)(2,1)}, bf16[64,8,256]{2,1,0:T(8,128)(2,1)}, u32[]{:S(2)}, u32[]{:S(2)}) collective-permute-start(bf16[64,8,256]{2,1,0:T(8,128)(2,1)} %get-tuple-element.80), channel_id=1, source_target_pairs={{0,2},{2,4},{4,6},{6,8},{8,10},{10,12},{12,14},{14,16},{16,18},{18... | collective-permute-start | bytes 786440 | tf_op jit(solution)/shard_map/ppermute | solution.py:22
  281.9 15.1 %collective-permute-start.9 = (bf16[64,8,256]{2,1,0:T(8,128)(2,1)}, bf16[64,8,256]{2,1,0:T(8,128)(2,1)}, u32[]{:S(2)}, u32[]{:S(2)}) collective-permute-start(bf16[64,8,256]{2,1,0:T(8,128)(2,1)} %get-tuple-element.81), channel_id=1, source_target_pairs={{2,0},{4,2},{6,4},{8,6},{10,8},{12,10},{14,12},{16,14},{18,16},{20... | collective-permute-start | bytes 786440 | tf_op jit(solution)/shard_map/ppermute | solution.py:24
  293.3 29.8 %collective-permute-start.21 = (f32[312,128]{1,0:T(8,128)}, f32[312,128]{1,0:T(8,128)}, u32[]{:S(2)}, u32[]{:S(2)}) collective-permute-start(f32[312,128]{1,0:T(8,128)} %pad_bitcast_fusion), channel_id=1, source_target_pairs={{0,2},{2,0},{4,6},{6,4},{8,10},{10,8},{12,14},{14,12},{16,18},{18,... | collective-permute-start | bytes 479240 | tf_op jit(solution)/shard_map/ppermute | solution.py:179
  302.0 35.0 %collective-permute-start.10 = (bf16[64,48,8]{0,2,1:T(8,128)(2,1)}, bf16[64,48,8]{0,2,1:T(8,128)(2,1)}, u32[]{:S(2)}, u32[]{:S(2)}) collective-permute-start(bf16[64,48,8]{0,2,1:T(8,128)(2,1)} %copy.417), channel_id=1, source_target_pairs={{0,1},{2,3},{4,5},{6,7},{8,9},{10,11},{12,13},{14,15},{16,17},{18,... | collective-permute-start | bytes 147464 | tf_op jit(solution)/shard_map/ppermute | solution.py:22
  321.8 17.5 %collective-permute-start.11 = (bf16[64,48,8]{0,2,1:T(8,128)(2,1)}, bf16[64,48,8]{0,2,1:T(8,128)(2,1)}, u32[]{:S(2)}, u32[]{:S(2)}) collective-permute-start(bf16[64,48,8]{0,2,1:T(8,128)(2,1)} %copy.418), channel_id=1, source_target_pairs={{1,0},{3,2},{5,4},{7,6},{9,8},{11,10},{13,12},{15,14},{17,16},{19,... | collective-permute-start | bytes 147464 | tf_op jit(solution)/shard_map/ppermute | solution.py:24
  324.8 67.3 %collective-permute-start.22 = (f32[312,128]{1,0:T(8,128)}, f32[312,128]{1,0:T(8,128)}, u32[]{:S(2)}, u32[]{:S(2)}) collective-permute-start(f32[312,128]{1,0:T(8,128)} %fusion.106), channel_id=1, source_target_pairs={{0,4},{2,6},{4,0},{6,2},{8,12},{10,14},{12,8},{14,10},{16,20},{18,... | collective-permute-start | bytes 479240 | tf_op jit(solution)/shard_map/ppermute | solution.py:179
  388.2 18.4 %copy-start.16 = (f32[36864]{0:T(1024)}, f32[36864]{0:T(1024)S(1)}, u32[]{:S(2)}) copy-start(f32[36864]{0:T(1024)S(1)} %reshape.104) | copy-start | bytes 442372
  388.3 10.6 %collective-permute-start.16 = (f32[296,128]{1,0:T(8,128)S(1)}, f32[296,128]{1,0:T(8,128)S(1)}, u32[]{:S(2)}, u32[]{:S(2)}) collective-permute-start(f32[296,128]{1,0:T(8,128)S(1)} %fusion.68), channel_id=1, source_target_pairs={{0,2},{2,0},{4,6},{6,4},{8,10},{10,8},{12,14},{14,12},{16,18},{18,... | collective-permute-start | bytes 454664 | tf_op jit(solution)/shard_map/ppermute | solution.py:179
  388.4 18.2 %collective-permute-start.12 = (bf16[64,8,256]{2,1,0:T(8,128)(2,1)S(1)}, bf16[64,8,256]{2,1,0:T(8,128)(2,1)S(1)}, u32[]{:S(2)}, u32[]{:S(2)}) collective-permute-start(bf16[64,8,256]{2,1,0:T(8,128)(2,1)S(1)} %get-tuple-element.78), channel_id=1, source_target_pairs={{0,2},{2,4},{4,6},{6,8},{8,10},{10,12},{12,14},{14,16},{16,18},{18... | collective-permute-start | bytes 786440 | tf_op jit(solution)/shard_map/ppermute | solution.py:22
  390.8 15.8 %collective-permute-start.13 = (bf16[64,8,256]{2,1,0:T(8,128)(2,1)S(1)}, bf16[64,8,256]{2,1,0:T(8,128)(2,1)S(1)}, u32[]{:S(2)}, u32[]{:S(2)}) collective-permute-start(bf16[64,8,256]{2,1,0:T(8,128)(2,1)S(1)} %get-tuple-element.79), channel_id=1, source_target_pairs={{2,0},{4,2},{6,4},{8,6},{10,8},{12,10},{14,12},{16,14},{18,16},{20... | collective-permute-start | bytes 786440 | tf_op jit(solution)/shard_map/ppermute | solution.py:24
  393.2 11.2 %collective-permute-start.23 = (f32[312,128]{1,0:T(8,128)S(1)}, f32[312,128]{1,0:T(8,128)S(1)}, u32[]{:S(2)}, u32[]{:S(2)}) collective-permute-start(f32[312,128]{1,0:T(8,128)S(1)} %fusion.138), channel_id=1, source_target_pairs={{0,8},{2,10},{4,12},{6,14},{8,0},{10,2},{12,4},{14,6},{16,24},{18,... | collective-permute-start | bytes 479240 | tf_op jit(solution)/shard_map/ppermute | solution.py:179
  399.6 18.0 %collective-permute-start.17 = (f32[296,128]{1,0:T(8,128)}, f32[296,128]{1,0:T(8,128)}, u32[]{:S(2)}, u32[]{:S(2)}) collective-permute-start(f32[296,128]{1,0:T(8,128)} %fusion.107), channel_id=1, source_target_pairs={{0,4},{2,6},{4,0},{6,2},{8,12},{10,14},{12,8},{14,10},{16,20},{18,... | collective-permute-start | bytes 454664 | tf_op jit(solution)/shard_map/ppermute | solution.py:179
  405.1 46.9 %collective-permute-start.24 = (f32[312,128]{1,0:T(8,128)}, f32[312,128]{1,0:T(8,128)}, u32[]{:S(2)}, u32[]{:S(2)}) collective-permute-start(f32[312,128]{1,0:T(8,128)} %add.100), channel_id=1, source_target_pairs={{0,16},{2,18},{4,20},{6,22},{8,24},{10,26},{12,28},{14,30},{16,0},... | collective-permute-start | bytes 479240 | tf_op jit(solution)/shard_map/ppermute | solution.py:179
  409.7 9.1 %collective-permute-start.14 = (bf16[64,48,8]{0,2,1:T(8,128)(2,1)S(1)}, bf16[64,48,8]{0,2,1:T(8,128)(2,1)S(1)}, u32[]{:S(2)}, u32[]{:S(2)}) collective-permute-start(bf16[64,48,8]{0,2,1:T(8,128)(2,1)S(1)} %copy.426), channel_id=1, source_target_pairs={{0,1},{2,3},{4,5},{6,7},{8,9},{10,11},{12,13},{14,15},{16,17},{18,... | collective-permute-start | bytes 147464 | tf_op jit(solution)/shard_map/ppermute | solution.py:22
  416.2 6.6 %collective-permute-start.15 = (bf16[64,48,8]{0,2,1:T(8,128)(2,1)S(1)}, bf16[64,48,8]{0,2,1:T(8,128)(2,1)S(1)}, u32[]{:S(2)}, u32[]{:S(2)}) collective-permute-start(bf16[64,48,8]{0,2,1:T(8,128)(2,1)S(1)} %copy.427), channel_id=1, source_target_pairs={{1,0},{3,2},{5,4},{7,6},{9,8},{11,10},{13,12},{15,14},{17,16},{19,... | collective-permute-start | bytes 147464 | tf_op jit(solution)/shard_map/ppermute | solution.py:24
  418.7 37.9 %collective-permute-start.18 = (f32[296,128]{1,0:T(8,128)S(1)}, f32[296,128]{1,0:T(8,128)}, u32[]{:S(2)}, u32[]{:S(2)}) collective-permute-start(f32[296,128]{1,0:T(8,128)S(1)} %fusion.139), channel_id=1, source_target_pairs={{0,8},{2,10},{4,12},{6,14},{8,0},{10,2},{12,4},{14,6},{16,24},{18,... | collective-permute-start | bytes 454664 | tf_op jit(solution)/shard_map/ppermute | solution.py:179
  453.0 5.3 %collective-permute-start.25 = (f32[312,128]{1,0:T(8,128)S(1)}, f32[312,128]{1,0:T(8,128)S(1)}, u32[]{:S(2)}, u32[]{:S(2)}) collective-permute-start(f32[312,128]{1,0:T(8,128)S(1)} %add.101), channel_id=1, source_target_pairs={{0,1},{1,0},{2,3},{3,2},{4,5},{5,4},{6,7},{7,6},{8,9},{9,8},{10,11... | collective-permute-start | bytes 479240 | tf_op jit(solution)/shard_map/ppermute | solution.py:179
  457.6 7.8 %collective-permute-start.19 = (f32[296,128]{1,0:T(8,128)S(1)}, f32[296,128]{1,0:T(8,128)S(1)}, u32[]{:S(2)}, u32[]{:S(2)}) collective-permute-start(f32[296,128]{1,0:T(8,128)S(1)} %add.95), channel_id=1, source_target_pairs={{0,16},{2,18},{4,20},{6,22},{8,24},{10,26},{12,28},{14,30},{16,0},... | collective-permute-start | bytes 454664 | tf_op jit(solution)/shard_map/ppermute | solution.py:179
  465.4 5.3 %collective-permute-start.20 = (f32[296,128]{1,0:T(8,128)S(1)}, f32[296,128]{1,0:T(8,128)S(1)}, u32[]{:S(2)}, u32[]{:S(2)}) collective-permute-start(f32[296,128]{1,0:T(8,128)S(1)} %add.96), channel_id=1, source_target_pairs={{0,1},{1,0},{2,3},{3,2},{4,5},{5,4},{6,7},{7,6},{8,9},{9,8},{10,11... | collective-permute-start | bytes 454664 | tf_op jit(solution)/shard_map/ppermute | solution.py:179
  (37 other events, 126.8 us)

commit v2 on v1

--- a/solution.py
+++ b/solution.py
@@ -37,19 +37,76 @@
 
 
 def with_rims(residual_block):
-    return with_halo(residual_block, (("ri", 1), ("rj", 2)), DILATION_RATE * (KERNEL_TAPS // 2))
+    return with_halo(residual_block, (("ri", 0), ("rj", 2)), DILATION_RATE * (KERNEL_TAPS // 2))
+
+
+def spread_taps(field, shifted):
+    rows, _, cols = shifted.shape
+    chans = field.shape[1]
+
+    @pl.loop(0, rows)
+    def _(row):
+        line = field[row]
+        for tap in range(KERNEL_TAPS):
+            start = DILATION_RATE * tap
+            shifted[row, chans * tap : chans * (tap + 1), :] = line[:, start : start + cols]
+
+
+def tap_stack(shifted, row):
+    return jnp.concatenate(
+        [shifted[row + DILATION_RATE * tap] for tap in range(KERNEL_TAPS)], axis=0
+    )
+
+
+def conv_kernel(field, weight, out, shifted):
+    spread_taps(field, shifted)
+
+    @pl.loop(0, out.shape[0])
+    def _(row):
+        out[row] = jnp.dot(
+            weight[...], tap_stack(shifted, row), preferred_element_type=jnp.float32
+        )
+
+
+def tap_kernel(field, grad, out, shifted):
+    spread_taps(field, shifted)
+    out[...] = jnp.zeros_like(out)
+
+    @pl.loop(0, grad.shape[0])
+    def _(row):
+        out[...] += lax.dot_general(
+            tap_stack(shifted, row),
+            grad[row],
+            (((1,), (1,)), ((), ())),
+            preferred_element_type=jnp.float32,
+        )
+
+
+def row_call(kernel, field, other, out_shape):
+    rows, chans, cols = field.shape
+    margin = DILATION_RATE * (KERNEL_TAPS - 1)
+    whole = pl.BlockSpec(memory_space=pltpu.VMEM)
+    flops = 2 * (rows - margin) * (cols - margin) * (KERNEL_TAPS * chans) ** 2
+    return pl.pallas_call(
+        kernel,
+        out_shape=jax.ShapeDtypeStruct(out_shape, jnp.float32),
+        in_specs=[whole, whole],
+        out_specs=whole,
+        scratch_shapes=[pltpu.VMEM((rows, KERNEL_TAPS * chans, cols - margin), jnp.bfloat16)],
+        cost_estimate=pl.CostEstimate(
+            flops=flops, bytes_accessed=4 * rows * chans * cols, transcendentals=0
+        ),
+        compiler_params=pltpu.CompilerParams(vmem_limit_bytes=40 * 1024 * 1024),
+    )(field, other)
 
 
 def dilated(padded_field, weight):
-    return lax.conv_general_dilated(
-        padded_field[None],
-        weight,
-        (1, 1),
-        [(0, 0), (0, 0)],
-        rhs_dilation=(DILATION_RATE, DILATION_RATE),
-        dimension_numbers=("NCHW", "HWIO", "NCHW"),
-        preferred_element_type=jnp.float32,
-    )[0]
+    rows, chans, cols = padded_field.shape
+    margin = DILATION_RATE * (KERNEL_TAPS - 1)
+    flat_weight = weight.reshape(-1, weight.shape[-1]).T
+    return row_call(
+        conv_kernel, padded_field, flat_weight, (rows - margin, flat_weight.shape[0], cols - margin)
+    )
 
 
 def flipped(weight):
@@ -57,22 +114,11 @@
 
 
 def tap_sums(padded_field, grad):
-    row_extent = grad.shape[1]
-    column_extent = grad.shape[2]
-    tap_rows = []
-    for row_stride in range(KERNEL_TAPS):
-        across = []
-        for column_stride in range(KERNEL_TAPS):
-            sliding_window = padded_field[
-                :,
-                DILATION_RATE * row_stride : DILATION_RATE * row_stride + row_extent,
-                DILATION_RATE * column_stride : DILATION_RATE * column_stride + column_extent,
-            ]
-            across.append(
-                jnp.einsum("cij,dij->cd", sliding_window, grad, preferred_element_type=jnp.float32)
-            )
-        tap_rows.append(jnp.stack(across))
-    return jnp.stack(tap_rows)
+    chans = padded_field.shape[1]
+    sums = row_call(
+        tap_kernel, padded_field, grad, (KERNEL_TAPS * KERNEL_TAPS * chans, grad.shape[1])
+    )
+    return sums.reshape(KERNEL_TAPS, KERNEL_TAPS, chans, grad.shape[1])
 
 
 def swap_kernel(count, src, dst, send_sem, recv_sem, own_sem):
@@ -163,12 +209,12 @@
 
 
 def mirror(block):
-    chan_count, row_count, col_count = block.shape
+    row_count, chan_count, col_count = block.shape
     count = col_count // row_count
-    parts = block.reshape(chan_count, row_count, count, row_count)
-    parts = jnp.transpose(parts, (2, 0, 3, 1)).reshape(count, -1, 128)
-    arrived = swapped(parts).reshape(count, chan_count, row_count, row_count)
-    return jnp.transpose(arrived, (1, 2, 0, 3)).reshape(chan_count, row_count, col_count)
+    parts = block.reshape(row_count, chan_count, count, row_count)
+    parts = jnp.transpose(parts, (2, 3, 1, 0)).reshape(count, -1, 128)
+    arrived = swapped(parts).reshape(count, row_count, chan_count, row_count)
+    return jnp.transpose(arrived, (1, 2, 0, 3)).reshape(row_count, chan_count, col_count)
 
 
 def summed_over_mesh(flat):
@@ -197,7 +243,8 @@
 def on_device(
     pair, conv1_weight, conv1_bias, conv2_weight, conv2_bias, head_weight, head_bias, bins, mask
 ):
-    row_count = pair.shape[1]
+    pair = jnp.transpose(pair, (1, 0, 2))
+    row_count = pair.shape[0]
     col_count = pair.shape[2]
     row_valid = lax.dynamic_slice_in_dim(mask, lax.axis_index("ri") * row_count, row_count).astype(
         jnp.float32
@@ -208,58 +255,58 @@
     pair_mask = row_valid[:, None] * col_valid[None, :]
     n_valid = jnp.sum(mask.astype(jnp.float32))
     pair_pad = with_rims(pair)
-    inner = dilated(pair_pad, conv1_weight) + conv1_bias[:, None, None]
+    inner = dilated(pair_pad, conv1_weight) + conv1_bias[:, None]
     inner_act = activate(inner).astype(jnp.bfloat16)
     act_pad = with_rims(inner_act)
-    outer = dilated(act_pad, conv2_weight) + conv2_bias[:, None, None]
+    outer = dilated(act_pad, conv2_weight) + conv2_bias[:, None]
     summed = pair.astype(jnp.float32) + outer
-    hidden = (pair_mask[None] * activate(summed)).astype(jnp.bfloat16)
-    bins_field = bins.astype(jnp.bfloat16)[None]
-    swapped_all = mirror(jnp.concatenate([hidden, bins_field], axis=0))
-    mirrored = swapped_all[:-1]
-    bins_mirrored = swapped_all[-1].astype(jnp.int32)
+    hidden = (pair_mask[:, None, :] * activate(summed)).astype(jnp.bfloat16)
+    bins_field = bins.astype(jnp.bfloat16)[:, None, :]
+    swapped_all = mirror(jnp.concatenate([hidden, bins_field], axis=1))
+    mirrored = swapped_all[:, :-1]
+    bins_mirrored = swapped_all[:, -1].astype(jnp.int32)
     logits = 0.5 * (
-        jnp.einsum("ck,cij->kij", head_weight, hidden, preferred_element_type=jnp.float32)
-        + jnp.einsum("ck,cij->kij", head_weight, mirrored, preferred_element_type=jnp.float32)
-    )
-    logits = logits + head_bias[:, None, None]
-    peak_logit = jnp.max(logits, axis=0, keepdims=True)
+        jnp.einsum("ck,icj->ikj", head_weight, hidden, preferred_element_type=jnp.float32)
+        + jnp.einsum("ck,icj->ikj", head_weight, mirrored, preferred_element_type=jnp.float32)
+    )
+    logits = logits + head_bias[:, None]
+    peak_logit = jnp.max(logits, axis=1, keepdims=True)
     powered = jnp.exp(logits - peak_logit)
-    chance = powered / jnp.sum(powered, axis=0, keepdims=True)
-    bin_ids = jnp.arange(head_weight.shape[1], dtype=jnp.int32)[:, None, None]
-    onehot = (bins[None] == bin_ids).astype(jnp.float32)
-    onehot_mirrored = (bins_mirrored[None] == bin_ids).astype(jnp.float32)
-    even_error = pair_mask[None] * (chance - 0.5 * (onehot + onehot_mirrored))
+    chance = powered / jnp.sum(powered, axis=1, keepdims=True)
+    bin_ids = jnp.arange(head_weight.shape[1], dtype=jnp.int32)[:, None]
+    onehot = (bins[:, None, :] == bin_ids).astype(jnp.float32)
+    onehot_mirrored = (bins_mirrored[:, None, :] == bin_ids).astype(jnp.float32)
+    even_error = pair_mask[:, None, :] * (chance - 0.5 * (onehot + onehot_mirrored))
     head_term = jnp.einsum(
-        "cij,kij->ck",
+        "icj,ikj->ck",
         hidden.astype(jnp.float32),
         even_error,
         precision=lax.Precision.HIGHEST,
         preferred_element_type=jnp.float32,
     )
-    head_bias_term = jnp.sum(even_error, axis=(1, 2))
+    head_bias_term = jnp.sum(even_error, axis=(0, 2))
     half_slope = jnp.einsum(
-        "ck,kij->cij",
+        "ck,ikj->icj",
         head_weight.astype(jnp.float32),
         even_error,
         precision=lax.Precision.HIGHEST,
         preferred_element_type=jnp.float32,
     )
-    outer_grad = half_slope * pair_mask[None] * activate_slope(summed)
+    outer_grad = half_slope * pair_mask[:, None, :] * activate_slope(summed)
     outer_half = outer_grad.astype(jnp.bfloat16)
     conv2_term = tap_sums(act_pad, outer_half)
-    conv2_bias_term = jnp.sum(outer_grad, axis=(1, 2))
+    conv2_bias_term = jnp.sum(outer_grad, axis=(0, 2))
     inner_grad = dilated(with_rims(outer_half), flipped(conv2_weight)) * activate_slope(inner)
     inner_half = inner_grad.astype(jnp.bfloat16)
     conv1_term = tap_sums(pair_pad, inner_half)
-    conv1_bias_term = jnp.sum(inner_grad, axis=(1, 2))
+    conv1_bias_term = jnp.sum(inner_grad, axis=(0, 2))
     grad_pair = (outer_grad + dilated(with_rims(inner_half), flipped(conv1_weight))).astype(
         jnp.bfloat16
     )
     late = sum_arrays((conv1_term, conv1_bias_term))
     early = sum_arrays((conv2_term, conv2_bias_term, head_term, head_bias_term))
     return (
-        grad_pair,
+        jnp.transpose(grad_pair, (1, 0, 2)),
         late[0] / n_valid,
         late[1] / n_valid,
         early[0] / n_valid,

time: 481 us -> 347 us (0.72); the launches traced: 474 us -> 345 us
  local copies, waits for them, and re-layouts: 171 us -> 75.5 us
  matrix products: 104 us -> 14.4 us
  Pallas kernels: 22.5 us -> 93.9 us
  other arithmetic: 70.8 us -> 35.9 us
  waiting for transfers between devices: 23.1 us -> 37.3 us
  starting transfers between devices: 80.6 us -> 86.7 us
    pallas_call x0 -> x6, Pallas kernels: none -> 67.3 us  [row_call(): pl.pallas_call(kernel, out_shape=jax.ShapeDtypeStruct(out_shape, jnp.floa...]
    conv_general_dilated x4 -> x0, matrix products: 54.9 us -> none  [dilated(): lax.conv_general_dilated(padded_field[None], weight, (1, 1), [(0, 0), (0,...]
    dot_general x21 -> x3, matrix products: 43.7 us -> 10.8 us  [the longest x1 6.34 us: on_device(): jnp.einsum('ck,ikj->icj', head_weight.astype(jnp.float32), even_error, pr...]
    broadcast_in_dim x2 -> x0, local copies, waits for them, and re-layouts: 31.3 us -> none  [dilated(): padded_field[None]]
    conv_general_dilated x10 -> x0, local copies, waits for them, and re-layouts: 28.6 us -> none  [dilated(): lax.conv_general_dilated(padded_field[None], weight, (1, 1), [(0, 0), (0,...]
    concatenate x4 -> x1, local copies, waits for them, and re-layouts: 18.9 us -> 5.29 us  [on_device(): swapped_all = mirror(jnp.concatenate([hidden, bins_field], axis=1))]
    ppermute x10, waiting for transfers between devices: 11 us -> 24.3 us  [summed_over_mesh(): lax.ppermute(flat, axis, [(i, i ^ stride) for i in range(size)])]
    slice x3 -> x0, local copies, waits for them, and re-layouts: 12.7 us -> none  [the longest x2 10.6 us: on_device(): mirrored = swapped_all[:-1]]
  transfers between devices with their start and end apart: 26 -> 26, of which waited for: 8 -> 11; matrix products, arithmetic and copies ran while one was open for 29% -> 9% of each run, Pallas kernels for 0% -> 10%
where the time goes in v2:
time: 347 us; the launch traced here: 345 us
  Pallas kernels  93.9 us (27%)
  starting transfers between devices  86.7 us (25%)
  local copies, waits for them, and re-layouts  75.5 us (22%)
  waiting for transfers between devices  37.3 us (11%)
  other arithmetic  35.9 us (10%)
  matrix products  14.4 us (4%)
    pallas_call x6, Pallas kernels, row_call(): pl.pallas_call(kernel, out_shape=jax.ShapeDtypeStruct(out_shape, jnp.floa...  67.3 us
    ppermute x8, starting transfers between devices, with_halo(): lax.ppermute(tail, axis, [(i, (i + 1) % count) for i in range(ends)])  49.1 us
    ppermute x10, starting transfers between devices, summed_over_mesh(): lax.ppermute(flat, axis, [(i, i ^ stride) for i in range(size)])  26.8 us
    pallas_call x1, Pallas kernels, swapped(): pl.pallas_call(functools.partial(swap_kernel, count), out_shape=jax.Shape...  26.6 us
    ppermute x10, waiting for transfers between devices, summed_over_mesh(): lax.ppermute(flat, axis, [(i, i ^ stride) for i in range(size)])  24.3 us
    concatenate x8, other arithmetic, with_halo(): jnp.concatenate([lax.ppermute(tail, axis, [(i, (i + 1) % count) for i in...  16 us
    ppermute x8, waiting for transfers between devices, with_halo(): lax.ppermute(head, axis, [((i + 1) % count, i) for i in range(ends)])  12.6 us
    unnamed x81, local copies, waits for them, and re-layouts  10.9 us
  transfers between devices with their start and end apart: 26, of which 11 were waited for; matrix products, arithmetic and copies ran while one was open for 9% of the time, Pallas kernels for 10%

profile of v2, /device:TPU:0, one launch (start us, length us, event | category | flops | bytes accessed | tf_op | source)
XLA Modules:
  0.0 345.2 jit_solution(1224674037898739819)
XLA Ops:
  6.9 3.5 %collective-permute-done.1 = bf16[8,64,256]{2,1,0:T(8,128)(2,1)S(1)} collective-permute-done((bf16[8,64,256]{2,1,0:T(8,128)(2,1)S(1)}, bf16[8,64,256]{2,1,0:T(8,128)(2,1)S(1)}, u32[]{:S(2)}, u32[]{:S(2)}) %collective-permute-start.1) | collective-permute-done | bytes 262176 | tf_op jit(solution)/shard_map/ppermute | solution.py:24
  12.1 3.4 collective-permute-start.2
  18.9 3.4 collective-permute-done.3
  26.9 10.8 %shard_map.144 = f32[32,64,256]{2,1,0:T(8,128)S(1)} custom-call(bf16[48,64,272]{2,1,0:T(8,128)(2,1)S(1)} %pad_maximum_fusion.field, bf16[64,576]{1,0:T(8,128)(2,1)S(1)} %bitcast.64), custom_call_target="tpu_custom_call" | custom-call | flops 603979776 | bytes 3342336 | tf_op jit(solution)/shard_map/pallas_call | solution.py:90
  39.1 5.2 %collective-permute-start.4 = (bf16[8,64,256]{2,1,0:T(8,128)(2,1)S(1)}, bf16[8,64,256]{2,1,0:T(8,128)(2,1)S(1)}, u32[]{:S(2)}, u32[]{:S(2)}) collective-permute-start(bf16[8,64,256]{2,1,0:T(8,128)(2,1)S(1)} %get-tuple-element.51), channel_id=1, source_target_pairs={{0,2},{2,4},{4,6},{6,8},{8,10},{10,12},{12,14},{14,16},{16,18},{18... | collective-permute-start | bytes 786440 | tf_op jit(solution)/shard_map/ppermute | solution.py:22
  56.9 5.3 %concatenate.51 = bf16[32,1,8,32]{1,3,2,0:T(8,128)(2,1)} reshape(bf16[32,256]{1,0:T(8,128)(2,1)S(1)} %convert_element_type.49) | data formatting | bytes 32768 | tf_op jit(solution)/shard_map/concatenate | solution.py:265
  70.2 10.8 %shard_map.145 = f32[32,64,256]{2,1,0:T(8,128)S(1)} custom-call(bf16[48,64,272]{2,1,0:T(8,128)(2,1)S(1)} %pad_maximum_fusion.1.field, bf16[64,576]{1,0:T(8,128)(2,1)S(1)} %bitcast.63), custom_call_target="tpu_custom_call" | custom-call | flops 603979776 | bytes 3342336 | tf_op jit(solution)/shard_map/pallas_call | solution.py:90
  85.5 4.8 %maximum_bitcast_fusion = bf16[8,32,65,32]{2,1,0,3:T(8,128)(2,1)} fusion(bf16[32,1,8,32]{1,3,2,0:T(8,128)(2,1)} %concatenate.51, bf16[32,64,8,32]{1,3,2,0:T(8,128)(2,1)} %bitcast.71), kind=kLoop, calls=%fused_computation.17 | loop fusion | flops 2129920 | bytes 2129920 | tf_op jit(solution)/shard_map/transpose | solution.py:215
  90.3 7.2 %copy.67 = bf16[8,32,65,32]{3,2,1,0:T(8,128)(2,1)} copy(bf16[8,32,65,32]{2,1,0,3:T(8,128)(2,1)} %maximum_bitcast_fusion) | data formatting | bytes 2129920 | tf_op jit(solution)/shard_map/transpose | solution.py:215
  97.5 5.4 %reshape.98.src = bf16[8,520,128]{2,1,0:T(8,128)(2,1)} reshape(bf16[8,32,65,32]{3,2,1,0:T(8,128)(2,1)} %copy.67) | data formatting | bytes 2129920 | tf_op jit(solution)/shard_map/reshape | solution.py:215
  102.9 26.6 %shard_map.146 = bf16[8,520,128]{2,1,0:T(8,128)(2,1)} custom-call(bf16[8,520,128]{2,1,0:T(8,128)(2,1)} %reshape.98.src), custom_call_target="tpu_custom_call" | custom-call | tf_op jit(solution)/shard_map/pallas_call | solution.py:197
  129.5 6.2 %reshape.99 = bf16[8,32,65,32]{3,2,1,0:T(8,128)(2,1)} reshape(bf16[8,520,128]{2,1,0:T(8,128)(2,1)} %shard_map.146) | data formatting | bytes 2129920 | tf_op jit(solution)/shard_map/reshape | solution.py:216
  135.7 6.0 %copy.68 = bf16[32,65,8,32]{1,3,2,0:T(8,128)(2,1)} copy(bf16[32,65,8,32]{3,1,0,2:T(8,128)(2,1)} %bitcast.65) | data formatting | bytes 2129920 | tf_op jit(solution)/shard_map/transpose | solution.py:217
  141.6 4.1 %convert_reduce_fusion = s32[32,256]{1,0:T(8,128)} fusion(bf16[32,65,256]{1,2,0:T(8,128)(2,1)} %bitcast.66), kind=kLoop, calls=%fused_computation.1 | loop fusion | flops 8192 | bytes 49152 | tf_op jit(solution)/shard_map/eq | solution.py:278
  148.1 3.6 %fusion.32 = (f32[32,256]{1,0:T(8,128)}, f32[32,37,256]{2,1,0:T(8,128)}) fusion(f32[32,256,37]{1,2,0:T(8,128)} %fusion.6, bf16[32,64,256]{2,1,0:T(8,128)(2,1)S(1)} %fusion.4, f32[37]{0:T(128)S(1)} %copy-done.37, bf16[64,37]{0,1:T(8,128)(2,1)S(1)} %copy-done), kind=kOutput, calls=%fused_computation.69 | convolution fusion | flops 40312868 | bytes 3511060 | tf_op jit(solution)/shard_map/sub | solution.py:274
  151.8 6.3 %fusion.33 = (bf16[32,64,256]{2,1,0:T(8,128)(2,1)S(1)}, f32[32,64,256]{2,1,0:T(8,128)}) fusion(f32[32,64,256]{2,1,0:T(8,128)} %copy-done.8, f32[64]{0:T(128)S(1)} %copy-done.38, bf16[64,32,256]{2,1,0:T(8,128)(2,1)} %param.9, f32[32,256]{1,0:T(8,128)S(1)} %broadcast_multiply_fusion, bf16[64,37]{0,1:T(8,128)(2,1)S(1)} %copy-done, ...), kind=kOutput, calls=%fused_computation.70 | convolution fusion | flops 240230400 | bytes 7639936 | tf_op jit(solution)/shard_map/ck,ikj->icj/dot_general | solution.py:288
  159.9 5.6 %collective-permute-start.8 = (bf16[8,64,256]{2,1,0:T(8,128)(2,1)}, bf16[8,64,256]{2,1,0:T(8,128)(2,1)}, u32[]{:S(2)}, u32[]{:S(2)}) collective-permute-start(bf16[8,64,256]{2,1,0:T(8,128)(2,1)} %get-tuple-element.49), channel_id=1, source_target_pairs={{0,2},{2,4},{4,6},{6,8},{8,10},{10,12},{12,14},{14,16},{16,18},{18... | collective-permute-start | bytes 786440 | tf_op jit(solution)/shard_map/ppermute | solution.py:22
  177.7 17.6 %collective-permute-start.10 = (bf16[48,64,8]{1,2,0:T(8,128)(2,1)}, bf16[48,64,8]{1,2,0:T(8,128)(2,1)}, u32[]{:S(2)}, u32[]{:S(2)}) collective-permute-start(bf16[48,64,8]{1,2,0:T(8,128)(2,1)} %copy.70), channel_id=1, source_target_pairs={{0,1},{2,3},{4,5},{6,7},{8,9},{10,11},{12,13},{14,15},{16,17},{18,... | collective-permute-start | bytes 147464 | tf_op jit(solution)/shard_map/ppermute | solution.py:22
  200.5 12.1 %shard_map.150 = f32[576,64]{1,0:T(8,128)S(1)} custom-call(bf16[48,64,272]{2,1,0:T(8,128)(2,1)S(1)} %copy-done.3, bf16[32,64,256]{2,1,0:T(8,128)(2,1)S(1)} %copy-done.7), custom_call_target="tpu_custom_call" | custom-call | flops 603979776 | bytes 3342336 | tf_op jit(solution)/shard_map/pallas_call | solution.py:90
  222.5 10.8 %shard_map.147 = f32[32,64,256]{2,1,0:T(8,128)S(1)} custom-call(bf16[48,64,272]{2,1,0:T(8,128)(2,1)S(1)} %pad_maximum_fusion.2.field, bf16[64,576]{1,0:T(8,128)(2,1)S(1)} %bitcast.62), custom_call_target="tpu_custom_call" | custom-call | flops 603979776 | bytes 3342336 | tf_op jit(solution)/shard_map/pallas_call | solution.py:90
  235.0 8.0 %collective-permute-start.12 = (bf16[8,64,256]{2,1,0:T(8,128)(2,1)}, bf16[8,64,256]{2,1,0:T(8,128)(2,1)}, u32[]{:S(2)}, u32[]{:S(2)}) collective-permute-start(bf16[8,64,256]{2,1,0:T(8,128)(2,1)} %get-tuple-element.47), channel_id=1, source_target_pairs={{0,2},{2,4},{4,6},{6,8},{8,10},{10,12},{12,14},{14,16},{16,18},{18... | collective-permute-start | bytes 786440 | tf_op jit(solution)/shard_map/ppermute | solution.py:22
  245.1 12.0 %shard_map.149 = f32[576,64]{1,0:T(8,128)S(1)} custom-call(bf16[48,64,272]{2,1,0:T(8,128)(2,1)S(1)} %pad_maximum_fusion.field, bf16[32,64,256]{2,1,0:T(8,128)(2,1)S(1)} %get-tuple-element.36.grad), custom_call_target="tpu_custom_call" | custom-call | flops 603979776 | bytes 3342336 | tf_op jit(solution)/shard_map/pallas_call | solution.py:90
  260.8 4.6 %collective-permute-start.14 = (bf16[48,64,8]{1,2,0:T(8,128)(2,1)S(1)}, bf16[48,64,8]{1,2,0:T(8,128)(2,1)S(1)}, u32[]{:S(2)}, u32[]{:S(2)}) collective-permute-start(bf16[48,64,8]{1,2,0:T(8,128)(2,1)S(1)} %copy.76), channel_id=1, source_target_pairs={{0,1},{2,3},{4,5},{6,7},{8,9},{10,11},{12,13},{14,15},{16,17},{18,... | collective-permute-start | bytes 147464 | tf_op jit(solution)/shard_map/ppermute | solution.py:22
  267.1 5.9 %collective-permute-start.16 = (f32[296,128]{1,0:T(8,128)S(1)}, f32[296,128]{1,0:T(8,128)S(1)}, u32[]{:S(2)}, u32[]{:S(2)}) collective-permute-start(f32[296,128]{1,0:T(8,128)S(1)} %fusion.14), channel_id=1, source_target_pairs={{0,2},{2,0},{4,6},{6,4},{8,10},{10,8},{12,14},{14,12},{16,18},{18,... | collective-permute-start | bytes 454664 | tf_op jit(solution)/shard_map/ppermute | solution.py:225
  277.8 10.8 %shard_map.148 = f32[32,64,256]{2,1,0:T(8,128)S(1)} custom-call(bf16[48,64,272]{2,1,0:T(8,128)(2,1)S(1)} %pad_maximum_fusion.3.field, bf16[64,576]{1,0:T(8,128)(2,1)S(1)} %bitcast.61), custom_call_target="tpu_custom_call" | custom-call | flops 603979776 | bytes 3342336 | tf_op jit(solution)/shard_map/pallas_call | solution.py:90
  289.6 3.8 %collective-permute-start.21 = (f32[312,128]{1,0:T(8,128)S(1)}, f32[312,128]{1,0:T(8,128)S(1)}, u32[]{:S(2)}, u32[]{:S(2)}) collective-permute-start(f32[312,128]{1,0:T(8,128)S(1)} %pad_bitcast_fusion), channel_id=1, source_target_pairs={{0,2},{2,0},{4,6},{6,4},{8,10},{10,8},{12,14},{14,12},{16,18},{18,... | collective-permute-start | bytes 479240 | tf_op jit(solution)/shard_map/ppermute | solution.py:225
  293.4 6.7 %collective-permute-start.17 = (f32[296,128]{1,0:T(8,128)S(1)}, f32[296,128]{1,0:T(8,128)S(1)}, u32[]{:S(2)}, u32[]{:S(2)}) collective-permute-start(f32[296,128]{1,0:T(8,128)S(1)} %fusion.19), channel_id=1, source_target_pairs={{0,4},{2,6},{4,0},{6,2},{8,12},{10,14},{12,8},{14,10},{16,20},{18,... | collective-permute-start | bytes 454664 | tf_op jit(solution)/shard_map/ppermute | solution.py:225
  301.5 3.4 collective-permute-done.17
  311.6 4.2 %collective-permute-start.19 = (f32[296,128]{1,0:T(8,128)S(1)}, f32[296,128]{1,0:T(8,128)S(1)}, u32[]{:S(2)}, u32[]{:S(2)}) collective-permute-start(f32[296,128]{1,0:T(8,128)S(1)} %add.95), channel_id=1, source_target_pairs={{0,16},{2,18},{4,20},{6,22},{8,24},{10,26},{12,28},{14,30},{16,0},... | collective-permute-start | bytes 454664 | tf_op jit(solution)/shard_map/ppermute | solution.py:225
  316.1 5.3 %collective-permute-done.19 = f32[296,128]{1,0:T(8,128)S(1)} collective-permute-done((f32[296,128]{1,0:T(8,128)S(1)}, f32[296,128]{1,0:T(8,128)S(1)}, u32[]{:S(2)}, u32[]{:S(2)}) %collective-permute-start.19) | collective-permute-done | bytes 151584 | tf_op jit(solution)/shard_map/ppermute | solution.py:225
  329.4 5.1 %collective-permute-done.24 = f32[312,128]{1,0:T(8,128)S(1)} collective-permute-done((f32[312,128]{1,0:T(8,128)S(1)}, f32[312,128]{1,0:T(8,128)S(1)}, u32[]{:S(2)}, u32[]{:S(2)}) %collective-permute-start.24) | collective-permute-done | bytes 159776 | tf_op jit(solution)/shard_map/ppermute | solution.py:225
  335.7 4.1 %collective-permute-done.25 = f32[312,128]{1,0:T(8,128)S(1)} collective-permute-done((f32[312,128]{1,0:T(8,128)S(1)}, f32[312,128]{1,0:T(8,128)S(1)}, u32[]{:S(2)}, u32[]{:S(2)}) %collective-permute-start.25) | collective-permute-done | bytes 159776 | tf_op jit(solution)/shard_map/ppermute | solution.py:225
  (195 shorter events, 111.1 us)
Async XLA Ops:
  0.6 145.1 %copy-start = (bf16[64,37]{0,1:T(8,128)(2,1)S(1)}, bf16[64,37]{0,1:T(8,128)(2,1)}, u32[]{:S(2)}) copy-start(bf16[64,37]{0,1:T(8,128)(2,1)} %param.14) | copy-start | bytes 14212
  2.6 4.4 %collective-permute-start = (bf16[8,64,256]{2,1,0:T(8,128)(2,1)S(1)}, bf16[8,64,256]{2,1,0:T(8,128)(2,1)S(1)}, u32[]{:S(2)}, u32[]{:S(2)}) collective-permute-start(bf16[8,64,256]{2,1,0:T(8,128)(2,1)S(1)} %get-tuple-element.53), channel_id=1, source_target_pairs={{0,2},{2,4},{4,6},{6,8},{8,10},{10,12},{12,14},{14,16},{16,18},{18... | collective-permute-start | bytes 786440 | tf_op jit(solution)/shard_map/ppermute | solution.py:22
  4.9 5.5 %collective-permute-start.1 = (bf16[8,64,256]{2,1,0:T(8,128)(2,1)S(1)}, bf16[8,64,256]{2,1,0:T(8,128)(2,1)S(1)}, u32[]{:S(2)}, u32[]{:S(2)}) collective-permute-start(bf16[8,64,256]{2,1,0:T(8,128)(2,1)S(1)} %get-tuple-element.54), channel_id=1, source_target_pairs={{2,0},{4,2},{6,4},{8,6},{10,8},{12,10},{14,12},{16,14},{18,16},{20... | collective-permute-start | bytes 786440 | tf_op jit(solution)/shard_map/ppermute | solution.py:24
  12.1 5.6 %collective-permute-start.2 = (bf16[48,64,8]{1,2,0:T(8,128)(2,1)S(1)}, bf16[48,64,8]{1,2,0:T(8,128)(2,1)S(1)}, u32[]{:S(2)}, u32[]{:S(2)}) collective-permute-start(bf16[48,64,8]{1,2,0:T(8,128)(2,1)S(1)} %copy.55), channel_id=1, source_target_pairs={{0,1},{2,3},{4,5},{6,7},{8,9},{10,11},{12,13},{14,15},{16,17},{18,... | collective-permute-start | bytes 147464 | tf_op jit(solution)/shard_map/ppermute | solution.py:22
  15.8 6.5 %collective-permute-start.3 = (bf16[48,64,8]{1,2,0:T(8,128)(2,1)S(1)}, bf16[48,64,8]{1,2,0:T(8,128)(2,1)S(1)}, u32[]{:S(2)}, u32[]{:S(2)}) collective-permute-start(bf16[48,64,8]{1,2,0:T(8,128)(2,1)S(1)} %copy.56), channel_id=1, source_target_pairs={{1,0},{3,2},{5,4},{7,6},{9,8},{11,10},{13,12},{15,14},{17,16},{19,... | collective-permute-start | bytes 147464 | tf_op jit(solution)/shard_map/ppermute | solution.py:24
  39.1 6.7 %collective-permute-start.4 = (bf16[8,64,256]{2,1,0:T(8,128)(2,1)S(1)}, bf16[8,64,256]{2,1,0:T(8,128)(2,1)S(1)}, u32[]{:S(2)}, u32[]{:S(2)}) collective-permute-start(bf16[8,64,256]{2,1,0:T(8,128)(2,1)S(1)} %get-tuple-element.51), channel_id=1, source_target_pairs={{0,2},{2,4},{4,6},{6,8},{8,10},{10,12},{12,14},{14,16},{16,18},{18... | collective-permute-start | bytes 786440 | tf_op jit(solution)/shard_map/ppermute | solution.py:22
  44.3 4.2 %collective-permute-start.5 = (bf16[8,64,256]{2,1,0:T(8,128)(2,1)S(1)}, bf16[8,64,256]{2,1,0:T(8,128)(2,1)S(1)}, u32[]{:S(2)}, u32[]{:S(2)}) collective-permute-start(bf16[8,64,256]{2,1,0:T(8,128)(2,1)S(1)} %get-tuple-element.52), channel_id=1, source_target_pairs={{2,0},{4,2},{6,4},{8,6},{10,8},{12,10},{14,12},{16,14},{18,16},{20... | collective-permute-start | bytes 786440 | tf_op jit(solution)/shard_map/ppermute | solution.py:24
  52.1 11.4 %collective-permute-start.6 = (bf16[48,64,8]{1,2,0:T(8,128)(2,1)}, bf16[48,64,8]{1,2,0:T(8,128)(2,1)}, u32[]{:S(2)}, u32[]{:S(2)}) collective-permute-start(bf16[48,64,8]{1,2,0:T(8,128)(2,1)} %copy.60), channel_id=1, source_target_pairs={{0,1},{2,3},{4,5},{6,7},{8,9},{10,11},{12,13},{14,15},{16,17},{18,... | collective-permute-start | bytes 147464 | tf_op jit(solution)/shard_map/ppermute | solution.py:22
  55.3 9.4 %collective-permute-start.7 = (bf16[48,64,8]{1,2,0:T(8,128)(2,1)}, bf16[48,64,8]{1,2,0:T(8,128)(2,1)}, u32[]{:S(2)}, u32[]{:S(2)}) collective-permute-start(bf16[48,64,8]{1,2,0:T(8,128)(2,1)} %copy.61), channel_id=1, source_target_pairs={{1,0},{3,2},{5,4},{7,6},{9,8},{11,10},{13,12},{15,14},{17,16},{19,... | collective-permute-start | bytes 147464 | tf_op jit(solution)/shard_map/ppermute | solution.py:24
  83.7 64.4 %copy-start.14 = (bf16[32,64,256]{2,1,0:T(8,128)(2,1)}, bf16[32,64,256]{2,1,0:T(8,128)(2,1)S(1)}, u32[]{:S(2)}) copy-start(bf16[32,64,256]{2,1,0:T(8,128)(2,1)S(1)} %fusion.4) | copy-start | bytes 3145732
  151.8 15.2 %copy-start.28 = (s32[32,256]{1,0:T(8,128)S(1)}, s32[32,256]{1,0:T(8,128)}, u32[]{:S(2)}) copy-start(s32[32,256]{1,0:T(8,128)} %convert_reduce_fusion) | copy-start | bytes 98308
  151.8 15.2 %copy-start.30 = (f32[32,256]{1,0:T(8,128)S(1)}, f32[32,256]{1,0:T(8,128)}, u32[]{:S(2)}) copy-start(f32[32,256]{1,0:T(8,128)} %get-tuple-element.55) | copy-start | bytes 98308
  151.8 15.2 %copy-start.33 = (s32[32,256]{1,0:T(8,128)S(1)}, s32[32,256]{1,0:T(8,128)}, u32[]{:S(2)}) copy-start(s32[32,256]{1,0:T(8,128)} %param.16) | copy-start | bytes 98308
  159.9 10.1 %collective-permute-start.8 = (bf16[8,64,256]{2,1,0:T(8,128)(2,1)}, bf16[8,64,256]{2,1,0:T(8,128)(2,1)}, u32[]{:S(2)}, u32[]{:S(2)}) collective-permute-start(bf16[8,64,256]{2,1,0:T(8,128)(2,1)} %get-tuple-element.49), channel_id=1, source_target_pairs={{0,2},{2,4},{4,6},{6,8},{8,10},{10,12},{12,14},{14,16},{16,18},{18... | collective-permute-start | bytes 786440 | tf_op jit(solution)/shard_map/ppermute | solution.py:22
  165.5 7.3 %collective-permute-start.9 = (bf16[8,64,256]{2,1,0:T(8,128)(2,1)}, bf16[8,64,256]{2,1,0:T(8,128)(2,1)}, u32[]{:S(2)}, u32[]{:S(2)}) collective-permute-start(bf16[8,64,256]{2,1,0:T(8,128)(2,1)} %get-tuple-element.50), channel_id=1, source_target_pairs={{2,0},{4,2},{6,4},{8,6},{10,8},{12,10},{14,12},{16,14},{18,16},{20... | collective-permute-start | bytes 786440 | tf_op jit(solution)/shard_map/ppermute | solution.py:24
  177.7 37.4 %collective-permute-start.10 = (bf16[48,64,8]{1,2,0:T(8,128)(2,1)}, bf16[48,64,8]{1,2,0:T(8,128)(2,1)}, u32[]{:S(2)}, u32[]{:S(2)}) collective-permute-start(bf16[48,64,8]{1,2,0:T(8,128)(2,1)} %copy.70), channel_id=1, source_target_pairs={{0,1},{2,3},{4,5},{6,7},{8,9},{10,11},{12,13},{14,15},{16,17},{18,... | collective-permute-start | bytes 147464 | tf_op jit(solution)/shard_map/ppermute | solution.py:22
  197.3 19.8 %collective-permute-start.11 = (bf16[48,64,8]{1,2,0:T(8,128)(2,1)}, bf16[48,64,8]{1,2,0:T(8,128)(2,1)}, u32[]{:S(2)}, u32[]{:S(2)}) collective-permute-start(bf16[48,64,8]{1,2,0:T(8,128)(2,1)} %copy.71), channel_id=1, source_target_pairs={{1,0},{3,2},{5,4},{7,6},{9,8},{11,10},{13,12},{15,14},{17,16},{19,... | collective-permute-start | bytes 147464 | tf_op jit(solution)/shard_map/ppermute | solution.py:24
  235.0 23.8 %collective-permute-start.12 = (bf16[8,64,256]{2,1,0:T(8,128)(2,1)}, bf16[8,64,256]{2,1,0:T(8,128)(2,1)}, u32[]{:S(2)}, u32[]{:S(2)}) collective-permute-start(bf16[8,64,256]{2,1,0:T(8,128)(2,1)} %get-tuple-element.47), channel_id=1, source_target_pairs={{0,2},{2,4},{4,6},{6,8},{8,10},{10,12},{12,14},{14,16},{16,18},{18... | collective-permute-start | bytes 786440 | tf_op jit(solution)/shard_map/ppermute | solution.py:22
  243.0 15.9 %collective-permute-start.13 = (bf16[8,64,256]{2,1,0:T(8,128)(2,1)}, bf16[8,64,256]{2,1,0:T(8,128)(2,1)}, u32[]{:S(2)}, u32[]{:S(2)}) collective-permute-start(bf16[8,64,256]{2,1,0:T(8,128)(2,1)} %get-tuple-element.48), channel_id=1, source_target_pairs={{2,0},{4,2},{6,4},{8,6},{10,8},{12,10},{14,12},{16,14},{18,16},{20... | collective-permute-start | bytes 786440 | tf_op jit(solution)/shard_map/ppermute | solution.py:24
  260.8 12.2 %collective-permute-start.14 = (bf16[48,64,8]{1,2,0:T(8,128)(2,1)S(1)}, bf16[48,64,8]{1,2,0:T(8,128)(2,1)S(1)}, u32[]{:S(2)}, u32[]{:S(2)}) collective-permute-start(bf16[48,64,8]{1,2,0:T(8,128)(2,1)S(1)} %copy.76), channel_id=1, source_target_pairs={{0,1},{2,3},{4,5},{6,7},{8,9},{10,11},{12,13},{14,15},{16,17},{18,... | collective-permute-start | bytes 147464 | tf_op jit(solution)/shard_map/ppermute | solution.py:22
  265.8 7.6 %collective-permute-start.15 = (bf16[48,64,8]{1,2,0:T(8,128)(2,1)S(1)}, bf16[48,64,8]{1,2,0:T(8,128)(2,1)}, u32[]{:S(2)}, u32[]{:S(2)}) collective-permute-start(bf16[48,64,8]{1,2,0:T(8,128)(2,1)S(1)} %copy.77), channel_id=1, source_target_pairs={{1,0},{3,2},{5,4},{7,6},{9,8},{11,10},{13,12},{15,14},{17,16},{19,... | collective-permute-start | bytes 147464 | tf_op jit(solution)/shard_map/ppermute | solution.py:24
  267.1 26.3 %collective-permute-start.16 = (f32[296,128]{1,0:T(8,128)S(1)}, f32[296,128]{1,0:T(8,128)S(1)}, u32[]{:S(2)}, u32[]{:S(2)}) collective-permute-start(f32[296,128]{1,0:T(8,128)S(1)} %fusion.14), channel_id=1, source_target_pairs={{0,2},{2,0},{4,6},{6,4},{8,10},{10,8},{12,14},{14,12},{16,18},{18,... | collective-permute-start | bytes 454664 | tf_op jit(solution)/shard_map/ppermute | solution.py:225
  289.6 10.5 %collective-permute-start.21 = (f32[312,128]{1,0:T(8,128)S(1)}, f32[312,128]{1,0:T(8,128)S(1)}, u32[]{:S(2)}, u32[]{:S(2)}) collective-permute-start(f32[312,128]{1,0:T(8,128)S(1)} %pad_bitcast_fusion), channel_id=1, source_target_pairs={{0,2},{2,0},{4,6},{6,4},{8,10},{10,8},{12,14},{14,12},{16,18},{18,... | collective-permute-start | bytes 479240 | tf_op jit(solution)/shard_map/ppermute | solution.py:225
  293.4 11.5 %collective-permute-start.17 = (f32[296,128]{1,0:T(8,128)S(1)}, f32[296,128]{1,0:T(8,128)S(1)}, u32[]{:S(2)}, u32[]{:S(2)}) collective-permute-start(f32[296,128]{1,0:T(8,128)S(1)} %fusion.19), channel_id=1, source_target_pairs={{0,4},{2,6},{4,0},{6,2},{8,12},{10,14},{12,8},{14,10},{16,20},{18,... | collective-permute-start | bytes 454664 | tf_op jit(solution)/shard_map/ppermute | solution.py:225
  300.1 15.7 %collective-permute-start.22 = (f32[312,128]{1,0:T(8,128)S(1)}, f32[312,128]{1,0:T(8,128)S(1)}, u32[]{:S(2)}, u32[]{:S(2)}) collective-permute-start(f32[312,128]{1,0:T(8,128)S(1)} %fusion.18), channel_id=1, source_target_pairs={{0,4},{2,6},{4,0},{6,2},{8,12},{10,14},{12,8},{14,10},{16,20},{18,... | collective-permute-start | bytes 479240 | tf_op jit(solution)/shard_map/ppermute | solution.py:225
  304.9 6.6 %collective-permute-start.18 = (f32[296,128]{1,0:T(8,128)S(1)}, f32[296,128]{1,0:T(8,128)S(1)}, u32[]{:S(2)}, u32[]{:S(2)}) collective-permute-start(f32[296,128]{1,0:T(8,128)S(1)} %fusion.39), channel_id=1, source_target_pairs={{0,8},{2,10},{4,12},{6,14},{8,0},{10,2},{12,4},{14,6},{16,24},{18,... | collective-permute-start | bytes 454664 | tf_op jit(solution)/shard_map/ppermute | solution.py:225
  311.6 9.8 %collective-permute-start.19 = (f32[296,128]{1,0:T(8,128)S(1)}, f32[296,128]{1,0:T(8,128)S(1)}, u32[]{:S(2)}, u32[]{:S(2)}) collective-permute-start(f32[296,128]{1,0:T(8,128)S(1)} %add.95), channel_id=1, source_target_pairs={{0,16},{2,18},{4,20},{6,22},{8,24},{10,26},{12,28},{14,30},{16,0},... | collective-permute-start | bytes 454664 | tf_op jit(solution)/shard_map/ppermute | solution.py:225
  315.8 10.8 %collective-permute-start.23 = (f32[312,128]{1,0:T(8,128)S(1)}, f32[312,128]{1,0:T(8,128)S(1)}, u32[]{:S(2)}, u32[]{:S(2)}) collective-permute-start(f32[312,128]{1,0:T(8,128)S(1)} %fusion.38), channel_id=1, source_target_pairs={{0,8},{2,10},{4,12},{6,14},{8,0},{10,2},{12,4},{14,6},{16,24},{18,... | collective-permute-start | bytes 479240 | tf_op jit(solution)/shard_map/ppermute | solution.py:225
  321.3 5.3 %collective-permute-start.20 = (f32[296,128]{1,0:T(8,128)S(1)}, f32[296,128]{1,0:T(8,128)S(1)}, u32[]{:S(2)}, u32[]{:S(2)}) collective-permute-start(f32[296,128]{1,0:T(8,128)S(1)} %add.96), channel_id=1, source_target_pairs={{0,1},{1,0},{2,3},{3,2},{4,5},{5,4},{6,7},{7,6},{8,9},{9,8},{10,11... | collective-permute-start | bytes 454664 | tf_op jit(solution)/shard_map/ppermute | solution.py:225
  322.0 23.2 %copy-start.1 = (bf16[64,37]{0,1:T(8,128)(2,1)S(1)}, bf16[64,37]{0,1:T(8,128)(2,1)}, u32[]{:S(2)}) copy-start(bf16[64,37]{0,1:T(8,128)(2,1)} %param.14) | copy-start | bytes 14212
  326.7 7.8 %collective-permute-start.24 = (f32[312,128]{1,0:T(8,128)S(1)}, f32[312,128]{1,0:T(8,128)S(1)}, u32[]{:S(2)}, u32[]{:S(2)}) collective-permute-start(f32[312,128]{1,0:T(8,128)S(1)} %add.100), channel_id=1, source_target_pairs={{0,16},{2,18},{4,20},{6,22},{8,24},{10,26},{12,28},{14,30},{16,0},... | collective-permute-start | bytes 479240 | tf_op jit(solution)/shard_map/ppermute | solution.py:225
  334.5 5.3 %collective-permute-start.25 = (f32[312,128]{1,0:T(8,128)S(1)}, f32[312,128]{1,0:T(8,128)S(1)}, u32[]{:S(2)}, u32[]{:S(2)}) collective-permute-start(f32[312,128]{1,0:T(8,128)S(1)} %add.101), channel_id=1, source_target_pairs={{0,1},{1,0},{2,3},{3,2},{4,5},{5,4},{6,7},{7,6},{8,9},{9,8},{10,11... | collective-permute-start | bytes 479240 | tf_op jit(solution)/shard_map/ppermute | solution.py:225
  (33 other events, 225.4 us)

commit v3 on v2

--- a/solution.py
+++ b/solution.py
@@ -121,7 +121,8 @@
     return sums.reshape(KERNEL_TAPS, KERNEL_TAPS, chans, grad.shape[1])
 
 
-def swap_kernel(count, src, dst, send_sem, recv_sem, own_sem):
+def swap_kernel(count, wide_src, small_src, wide_dst, small_dst, send_sem, recv_sem, own_sem):
+    lanes = ((0, wide_src, wide_dst), (1, small_src, small_dst))
     row = lax.axis_index("ri")
     column = lax.axis_index("rj")
     slot = lax.rem(row, count)
@@ -132,22 +133,22 @@
     def meets_self(block):
         return jnp.logical_and(own_group, slot == block)
 
-    def exchange(block):
+    def exchange(lane, src, dst, block):
         return pltpu.make_async_remote_copy(
             src_ref=src.at[block],
             dst_ref=dst.at[slot],
-            send_sem=send_sem.at[block],
-            recv_sem=recv_sem.at[slot],
+            send_sem=send_sem.at[lane, block],
+            recv_sem=recv_sem.at[lane, slot],
             device_id=(count * column + block, far_column),
             device_id_type=pl.DeviceIdType.MESH,
         )
 
-    def arrival(block):
+    def arrival(lane, src, dst, block):
         return pltpu.make_async_remote_copy(
             src_ref=src.at[block],
             dst_ref=dst.at[block],
-            send_sem=send_sem.at[block],
-            recv_sem=recv_sem.at[block],
+            send_sem=send_sem.at[lane, block],
+            recv_sem=recv_sem.at[lane, block],
             device_id=(count * column + block, far_column),
             device_id_type=pl.DeviceIdType.MESH,
         )
@@ -175,62 +176,162 @@
 
         @pl.when(jnp.logical_not(meets_self(block)))
         def _():
-            exchange(block).start()
+            for part in lanes:
+                exchange(*part, block).start()
 
         @pl.when(meets_self(block))
         def _():
-            pltpu.make_async_copy(src.at[block], dst.at[block], own_sem).start()
+            for lane, src, dst in lanes:
+                pltpu.make_async_copy(src.at[block], dst.at[block], own_sem.at[lane]).start()
 
     for block in range(count):
 
         @pl.when(jnp.logical_not(meets_self(block)))
         def _():
-            arrival(block).wait()
+            for part in lanes:
+                arrival(*part, block).wait()
 
         @pl.when(meets_self(block))
         def _():
-            pltpu.make_async_copy(src.at[block], dst.at[block], own_sem).wait()
-
-
-def swapped(blocks):
-    count = blocks.shape[0]
+            for lane, src, dst in lanes:
+                pltpu.make_async_copy(src.at[block], dst.at[block], own_sem.at[lane]).wait()
+
+
+def swapped(wide, small):
+    count = wide.shape[0]
+    anywhere = pl.BlockSpec(memory_space=pl.ANY)
     return pl.pallas_call(
         functools.partial(swap_kernel, count),
-        out_shape=jax.ShapeDtypeStruct(blocks.shape, blocks.dtype),
-        in_specs=[pl.BlockSpec(memory_space=pl.ANY)],
-        out_specs=pl.BlockSpec(memory_space=pl.ANY),
+        out_shape=[jax.ShapeDtypeStruct(a.shape, a.dtype) for a in (wide, small)],
+        in_specs=[anywhere, anywhere],
+        out_specs=[anywhere, anywhere],
         scratch_shapes=[
-            pltpu.SemaphoreType.DMA((count,)),
-            pltpu.SemaphoreType.DMA((count,)),
-            pltpu.SemaphoreType.DMA,
+            pltpu.SemaphoreType.DMA((2, count)),
+            pltpu.SemaphoreType.DMA((2, count)),
+            pltpu.SemaphoreType.DMA((2,)),
         ],
         compiler_params=pltpu.CompilerParams(collective_id=0, has_side_effects=True),
+    )(wide, small)
+
+
+def mirror(field, labels):
+    rows, chans, cols = field.shape
+    count = cols // rows
+    half = rows // 2
+    wide = jnp.concatenate([field[:half], field[half:]], axis=1)
+    wide = jnp.transpose(wide.reshape(half, 2 * chans, count, rows), (2, 3, 0, 1))
+    small = jnp.transpose(labels.reshape(rows, count, rows), (1, 2, 0))
+    wide, small = swapped(
+        wide.reshape(count, rows * half, 2 * chans), small.reshape(count, -1, 128)
+    )
+    wide = wide.reshape(count, rows, half, 2 * chans)
+    wide = jnp.concatenate([wide[..., :chans], wide[..., chans:]], axis=2)
+    field = jnp.transpose(wide, (1, 3, 0, 2)).reshape(rows, chans, cols)
+    labels = jnp.transpose(small.reshape(count, rows, rows), (1, 0, 2)).reshape(rows, cols)
+    return field, labels
+
+
+def sum_kernel(
+    row_axis, column_axis, own, out, slots, middle, whole,
+    send_one, recv_one, send_two, recv_two, send_three, recv_three,
+):
+    row = lax.axis_index("ri")
+    column = lax.axis_index("rj")
+    barrier = pltpu.get_barrier_semaphore()
+    row_peers = [(step, lax.rem(row + step, row_axis)) for step in range(1, row_axis)]
+    column_peers = [(step, lax.rem(column + step, column_axis)) for step in range(1, column_axis)]
+    for _, peer in row_peers:
+        pl.semaphore_signal(
+            barrier, inc=1, device_id=(peer, column), device_id_type=pl.DeviceIdType.MESH
+        )
+    for _, peer in column_peers:
+        pl.semaphore_signal(
+            barrier, inc=1, device_id=(row, peer), device_id_type=pl.DeviceIdType.MESH
+        )
+    pl.semaphore_wait(barrier, row_axis + column_axis - 2)
+
+    def exchange(copies):
+        for copy in copies:
+            copy.start()
+        for copy in copies:
+            copy.wait()
+
+    exchange(
+        [
+            pltpu.make_async_remote_copy(
+                src_ref=own.at[peer],
+                dst_ref=slots.at[step],
+                send_sem=send_one.at[step],
+                recv_sem=recv_one.at[step],
+                device_id=(peer, column),
+                device_id_type=pl.DeviceIdType.MESH,
+            )
+            for step, peer in row_peers
+        ]
+    )
+    total = own[row]
+    for step, _ in row_peers:
+        total = total + slots[step]
+    middle[column] = total
+    exchange(
+        [
+            pltpu.make_async_remote_copy(
+                src_ref=middle.at[column],
+                dst_ref=middle.at[column],
+                send_sem=send_two.at[step],
+                recv_sem=recv_two.at[step],
+                device_id=(row, peer),
+                device_id_type=pl.DeviceIdType.MESH,
+            )
+            for step, peer in column_peers
+        ]
+    )
+    total = middle[0]
+    for index in range(1, column_axis):
+        total = total + middle[index]
+    whole[row] = total
+    exchange(
+        [
+            pltpu.make_async_remote_copy(
+                src_ref=whole.at[row],
+                dst_ref=whole.at[row],
+                send_sem=send_three.at[step],
+                recv_sem=recv_three.at[step],
+                device_id=(peer, column),
+                device_id_type=pl.DeviceIdType.MESH,
+            )
+            for step, peer in row_peers
+        ]
+    )
+    out[...] = whole[...]
+
+
+def summed_over_mesh(blocks):
+    row_axis = lax.axis_size("ri")
+    column_axis = lax.axis_size("rj")
+    in_vmem = pl.BlockSpec(memory_space=pltpu.VMEM)
+    return pl.pallas_call(
+        functools.partial(sum_kernel, row_axis, column_axis),
+        out_shape=jax.ShapeDtypeStruct(blocks.shape, blocks.dtype),
+        in_specs=[in_vmem],
+        out_specs=in_vmem,
+        scratch_shapes=[
+            pltpu.VMEM(blocks.shape, blocks.dtype),
+            pltpu.VMEM((column_axis,) + blocks.shape[1:], blocks.dtype),
+            pltpu.VMEM(blocks.shape, blocks.dtype),
+        ]
+        + [
+            pltpu.SemaphoreType.DMA((size,))
+            for size in (row_axis, row_axis, column_axis, column_axis, row_axis, row_axis)
+        ],
+        compiler_params=pltpu.CompilerParams(collective_id=1, has_side_effects=True),
     )(blocks)
-
-
-def mirror(block):
-    row_count, chan_count, col_count = block.shape
-    count = col_count // row_count
-    parts = block.reshape(row_count, chan_count, count, row_count)
-    parts = jnp.transpose(parts, (2, 3, 1, 0)).reshape(count, -1, 128)
-    arrived = swapped(parts).reshape(count, row_count, chan_count, row_count)
-    return jnp.transpose(arrived, (1, 2, 0, 3)).reshape(row_count, chan_count, col_count)
-
-
-def summed_over_mesh(flat):
-    for axis in ("ri", "rj"):
-        size = lax.axis_size(axis)
-        stride = 1
-        while stride < size:
-            flat = flat + lax.ppermute(flat, axis, [(i, i ^ stride) for i in range(size)])
-            stride *= 2
-    return flat
 
 
 def sum_arrays(arrays):
     flat = jnp.concatenate([a.reshape(-1) for a in arrays])
-    used = flat.shape[0]
-    flat = jnp.pad(flat, (0, -used % 1024)).reshape(-1, 128)
+    parts = lax.axis_size("ri")
+    flat = jnp.pad(flat, (0, -flat.shape[0] % (parts * 1024))).reshape(parts, -1, 128)
     flat = summed_over_mesh(flat).reshape(-1)
     outs = []
     start = 0
@@ -261,10 +362,8 @@
     outer = dilated(act_pad, conv2_weight) + conv2_bias[:, None]
     summed = pair.astype(jnp.float32) + outer
     hidden = (pair_mask[:, None, :] * activate(summed)).astype(jnp.bfloat16)
-    bins_field = bins.astype(jnp.bfloat16)[:, None, :]
-    swapped_all = mirror(jnp.concatenate([hidden, bins_field], axis=1))
-    mirrored = swapped_all[:, :-1]
-    bins_mirrored = swapped_all[:, -1].astype(jnp.int32)
+    mirrored, bins_mirrored = mirror(hidden, bins.astype(jnp.bfloat16))
+    bins_mirrored = bins_mirrored.astype(jnp.int32)
     logits = 0.5 * (
         jnp.einsum("ck,icj->ikj", head_weight, hidden, preferred_element_type=jnp.float32)
         + jnp.einsum("ck,icj->ikj", head_weight, mirrored, preferred_element_type=jnp.float32)
@@ -303,17 +402,10 @@
     grad_pair = (outer_grad + dilated(with_rims(inner_half), flipped(conv1_weight))).astype(
         jnp.bfloat16
     )
-    late = sum_arrays((conv1_term, conv1_bias_term))
-    early = sum_arrays((conv2_term, conv2_bias_term, head_term, head_bias_term))
-    return (
-        jnp.transpose(grad_pair, (1, 0, 2)),
-        late[0] / n_valid,
-        late[1] / n_valid,
-        early[0] / n_valid,
-        early[1] / n_valid,
-        early[2] / n_valid,
-        early[3] / n_valid,
-    )
+    totals = sum_arrays(
+        (conv1_term, conv1_bias_term, conv2_term, conv2_bias_term, head_term, head_bias_term)
+    )
+    return (jnp.transpose(grad_pair, (1, 0, 2)), *[total / n_valid for total in totals])
 
 
 def solution(mesh):

time: 347 us -> 321 us (0.925)
  Pallas kernels: 93.9 us -> 123 us
  starting transfers between devices: 86.7 us -> 62.9 us
  waiting for transfers between devices: 37.3 us -> 18.6 us
  local copies, waits for them, and re-layouts: 75.5 us -> 67.2 us
  other arithmetic: 35.9 us -> 30.3 us
    pallas_call x1 -> x2, Pallas kernels: 26.6 us -> 55.6 us  [the longest x1 29 us: summed_over_mesh(): pl.pallas_call(functools.partial(sum_kernel, row_axis, column_axis), out_...]
    ppermute x10 -> x0, starting transfers between devices: 26.8 us -> none  [summed_over_mesh(): lax.ppermute(flat, axis, [(i, i ^ stride) for i in range(size)])]
    ppermute x10 -> x0, waiting for transfers between devices: 24.3 us -> none  [summed_over_mesh(): lax.ppermute(flat, axis, [(i, i ^ stride) for i in range(size)])]
    reshape x3 -> x2, local copies, waits for them, and re-layouts: 11.5 us -> 0.84 us  [the longest x1 0.72 us: mirror(): small.reshape(count, -1, 128)]
    transpose x2 -> x1, local copies, waits for them, and re-layouts: 13.2 us -> 2.62 us  [mirror(): jnp.transpose(wide.reshape(half, 2 * chans, count, rows), (2, 3, 0, 1))]
    ppermute x8, waiting for transfers between devices: 12.6 us -> 17.5 us  [with_halo(): lax.ppermute(head, axis, [((i + 1) % count, i) for i in range(ends)])]
    transpose x1 -> x0, other arithmetic: 4.8 us -> none  [mirror(): parts = jnp.transpose(parts, (2, 3, 1, 0)).reshape(count, -1, 128)]
    concatenate x1, local copies, waits for them, and re-layouts: 5.29 us -> 0.56 us  [mirror(): wide = jnp.concatenate([wide[..., :chans], wide[..., chans:]], axis=2)]
  transfers between devices with their start and end apart: 26 -> 16, of which waited for: 11 -> 5; matrix products, arithmetic and copies ran while one was open for 9% -> 6% of each run, Pallas kernels for 10% -> 8%
where the time goes in v3:
time: 321 us; the launch traced here: 318 us
  Pallas kernels  123 us (38%)
  local copies, waits for them, and re-layouts  67.2 us (21%)
  starting transfers between devices  62.9 us (20%)
  other arithmetic  30.3 us (9%)
  waiting for transfers between devices  18.6 us (6%)
  matrix products  14.4 us (4%)
    pallas_call x6, Pallas kernels, row_call(): pl.pallas_call(kernel, out_shape=jax.ShapeDtypeStruct(out_shape, jnp.floa...  67.3 us
    ppermute x8, starting transfers between devices, with_halo(): lax.ppermute(tail, axis, [(i, (i + 1) % count) for i in range(ends)])  52.3 us
    pallas_call x1, Pallas kernels, summed_over_mesh(): pl.pallas_call(functools.partial(sum_kernel, row_axis, column_axis), out_...  29 us
    pallas_call x1, Pallas kernels, swapped(): pl.pallas_call(functools.partial(swap_kernel, count), out_shape=[jax.Shap...  26.6 us
    ppermute x8, waiting for transfers between devices, with_halo(): lax.ppermute(head, axis, [((i + 1) % count, i) for i in range(ends)])  17.5 us
    concatenate x8, other arithmetic, with_halo(): jnp.concatenate([lax.ppermute(tail, axis, [(i, (i + 1) % count) for i in...  15.2 us
    slice x12, local copies, waits for them, and re-layouts, with_halo(): lax.slice_in_dim(cells, cells.shape[dim] - width, cells.shape[dim], axis=...  14.2 us
    ppermute x8, starting transfers between devices, with_halo(): lax.ppermute(head, axis, [((i + 1) % count, i) for i in range(ends)])  10.6 us
  transfers between devices with their start and end apart: 16, of which 5 were waited for; matrix products, arithmetic and copies ran while one was open for 6% of the time, Pallas kernels for 8%

profile of v3, /device:TPU:0, one launch (start us, length us, event | category | flops | bytes accessed | tf_op | source)
XLA Modules:
  0.0 317.6 jit_solution(7973365247729514868)
XLA Ops:
  2.6 2.4 collective-permute-start
  7.6 2.9 collective-permute-done.1
  15.7 4.6 %collective-permute-start.2 = (bf16[48,64,8]{1,2,0:T(8,128)(2,1)S(1)}, bf16[48,64,8]{1,2,0:T(8,128)(2,1)S(1)}, u32[]{:S(2)}, u32[]{:S(2)}) collective-permute-start(bf16[48,64,8]{1,2,0:T(8,128)(2,1)S(1)} %copy.43), channel_id=1, source_target_pairs={{0,1},{2,3},{4,5},{6,7},{8,9},{10,11},{12,13},{14,15},{16,17},{18,... | collective-permute-start | bytes 147464 | tf_op jit(solution)/shard_map/ppermute | solution.py:22
  24.9 3.3 %pad_maximum_fusion.field = bf16[48,64,272]{2,1,0:T(8,128)(2,1)S(1)} fusion(bf16[48,64,8]{2,1,0:T(8,128)(2,1)} %copy.46, bf16[8,64,256]{2,1,0:T(8,128)(2,1)} %copy-done.20, bf16[32,64,256]{2,1,0:T(8,128)(2,1)S(1)} %bitcast.66, bf16[8,64,256]{2,1,0:T(8,128)(2,1)} %copy-done.19, bf16[48,64,8]{2,1,0:T(8,128)(2,1)} %copy.45), kind=kLoop, calls=%fused_computation.5 | loop fusion | flops 8355840 | bytes 3342336 | tf_op jit(solution)/shard_map/concatenate | solution.py:20
  28.2 10.8 %shard_map.144 = f32[32,64,256]{2,1,0:T(8,128)S(1)} custom-call(bf16[48,64,272]{2,1,0:T(8,128)(2,1)S(1)} %pad_maximum_fusion.field, bf16[64,576]{1,0:T(8,128)(2,1)S(1)} %bitcast.63), custom_call_target="tpu_custom_call" | custom-call | flops 603979776 | bytes 3342336 | tf_op jit(solution)/shard_map/pallas_call | solution.py:90
  40.4 5.5 %collective-permute-start.4 = (bf16[8,64,256]{2,1,0:T(8,128)(2,1)S(1)}, bf16[8,64,256]{2,1,0:T(8,128)(2,1)S(1)}, u32[]{:S(2)}, u32[]{:S(2)}) collective-permute-start(bf16[8,64,256]{2,1,0:T(8,128)(2,1)S(1)} %get-tuple-element.52), channel_id=1, source_target_pairs={{0,2},{2,4},{4,6},{6,8},{8,10},{10,12},{12,14},{14,16},{16,18},{18... | collective-permute-start | bytes 786440 | tf_op jit(solution)/shard_map/ppermute | solution.py:22
  47.4 2.4 collective-permute-done.5
  51.4 2.1 copy.48
  55.7 5.8 %collective-permute-start.6 = (bf16[48,64,8]{1,2,0:T(8,128)(2,1)}, bf16[48,64,8]{1,2,0:T(8,128)(2,1)}, u32[]{:S(2)}, u32[]{:S(2)}) collective-permute-start(bf16[48,64,8]{1,2,0:T(8,128)(2,1)} %copy.48), channel_id=1, source_target_pairs={{0,1},{2,3},{4,5},{6,7},{8,9},{10,11},{12,13},{14,15},{16,17},{18,... | collective-permute-start | bytes 147464 | tf_op jit(solution)/shard_map/ppermute | solution.py:22
  66.5 2.1 copy.51
  68.6 3.3 %pad_maximum_fusion.1.field = bf16[48,64,272]{2,1,0:T(8,128)(2,1)S(1)} fusion(bf16[48,64,8]{2,1,0:T(8,128)(2,1)} %copy.51, bf16[8,64,256]{2,1,0:T(8,128)(2,1)} %copy-done.22, bf16[32,64,256]{2,1,0:T(8,128)(2,1)} %copy-done.12, bf16[8,64,256]{2,1,0:T(8,128)(2,1)} %copy-done.21, bf16[48,64,8]{2,1,0:T(8,128)(2,1)S(1)} %copy.50), kind=kLoop, calls=%fused_computation.6 | loop fusion | flops 8355840 | bytes 3342336 | tf_op jit(solution)/shard_map/concatenate | solution.py:20
  72.0 10.8 %shard_map.145 = f32[32,64,256]{2,1,0:T(8,128)S(1)} custom-call(bf16[48,64,272]{2,1,0:T(8,128)(2,1)S(1)} %pad_maximum_fusion.1.field, bf16[64,576]{1,0:T(8,128)(2,1)S(1)} %bitcast.62), custom_call_target="tpu_custom_call" | custom-call | flops 603979776 | bytes 3342336 | tf_op jit(solution)/shard_map/pallas_call | solution.py:90
  85.5 2.6 copy.77
  88.2 26.6 %shard_map.146 = (bf16[8,512,128]{2,1,0:T(8,128)(2,1)}, bf16[8,8,128]{2,1,0:T(8,128)(2,1)}) custom-call(bf16[8,512,128]{2,1,0:T(8,128)(2,1)} %bitcast.69, bf16[8,8,128]{2,1,0:T(8,128)(2,1)} %reshape.107.small_src), custom_call_target="tpu_custom_call" | custom-call | tf_op jit(solution)/shard_map/pallas_call | solution.py:203
  124.0 2.4 fusion.13
  126.4 3.6 %fusion.30 = (f32[32,256]{1,0:T(8,128)}, f32[32,37,256]{2,1,0:T(8,128)}) fusion(f32[32,256,37]{1,2,0:T(8,128)} %fusion.13, bf16[32,64,256]{2,1,0:T(8,128)(2,1)S(1)} %fusion.4, f32[37]{0:T(128)S(1)} %copy-done.40, bf16[64,37]{0,1:T(8,128)(2,1)S(1)} %copy-done), kind=kOutput, calls=%fused_computation.65 | convolution fusion | flops 40312868 | bytes 3511060 | tf_op jit(solution)/shard_map/sub | solution.py:373
  130.0 6.3 %fusion.31 = (bf16[32,64,256]{2,1,0:T(8,128)(2,1)S(1)}, f32[32,64,256]{2,1,0:T(8,128)}) fusion(f32[32,64,256]{2,1,0:T(8,128)} %copy-done.8, f32[64]{0:T(128)S(1)} %copy-done.41, bf16[64,32,256]{2,1,0:T(8,128)(2,1)} %param.9, f32[32,256]{1,0:T(8,128)S(1)} %broadcast_multiply_fusion, bf16[64,37]{0,1:T(8,128)(2,1)S(1)} %copy-done, ...), kind=kOutput, calls=%fused_computation.66 | convolution fusion | flops 240230400 | bytes 7639936 | tf_op jit(solution)/shard_map/ck,ikj->icj/dot_general | solution.py:387
  138.2 5.3 %collective-permute-start.8 = (bf16[8,64,256]{2,1,0:T(8,128)(2,1)}, bf16[8,64,256]{2,1,0:T(8,128)(2,1)}, u32[]{:S(2)}, u32[]{:S(2)}) collective-permute-start(bf16[8,64,256]{2,1,0:T(8,128)(2,1)} %get-tuple-element.46), channel_id=1, source_target_pairs={{0,2},{2,4},{4,6},{6,8},{8,10},{10,12},{12,14},{14,16},{16,18},{18... | collective-permute-start | bytes 786440 | tf_op jit(solution)/shard_map/ppermute | solution.py:22
  147.9 2.6 collective-permute-done.9
  158.6 15.6 %collective-permute-start.10 = (bf16[48,64,8]{1,2,0:T(8,128)(2,1)}, bf16[48,64,8]{1,2,0:T(8,128)(2,1)}, u32[]{:S(2)}, u32[]{:S(2)}) collective-permute-start(bf16[48,64,8]{1,2,0:T(8,128)(2,1)} %copy.60), channel_id=1, source_target_pairs={{0,1},{2,3},{4,5},{6,7},{8,9},{10,11},{12,13},{14,15},{16,17},{18,... | collective-permute-start | bytes 147464 | tf_op jit(solution)/shard_map/ppermute | solution.py:22
  175.9 12.1 %shard_map.150 = f32[576,64]{1,0:T(8,128)S(1)} custom-call(bf16[48,64,272]{2,1,0:T(8,128)(2,1)S(1)} %copy-done.3, bf16[32,64,256]{2,1,0:T(8,128)(2,1)S(1)} %copy-done.7), custom_call_target="tpu_custom_call" | custom-call | flops 603979776 | bytes 3342336 | tf_op jit(solution)/shard_map/pallas_call | solution.py:90
  192.4 2.1 copy.63
  194.5 3.4 %pad_maximum_fusion.2.field = bf16[48,64,272]{2,1,0:T(8,128)(2,1)S(1)} fusion(bf16[48,64,8]{2,1,0:T(8,128)(2,1)} %copy.63, bf16[8,64,256]{2,1,0:T(8,128)(2,1)} %collective-permute-done.9, bf16[32,64,256]{2,1,0:T(8,128)(2,1)S(1)} %copy-done.7, bf16[8,64,256]{2,1,0:T(8,128)(2,1)} %collective-permute-done.8, bf16[48,64,8]{2,1,0:T(8,128)(2,1)} %copy.62), kind=kLoop, calls=%fused_computation.7 | loop fusion | flops 8355840 | bytes 3342336 | tf_op jit(solution)/shard_map/concatenate | solution.py:20
  197.9 10.8 %shard_map.147 = f32[32,64,256]{2,1,0:T(8,128)S(1)} custom-call(bf16[48,64,272]{2,1,0:T(8,128)(2,1)S(1)} %pad_maximum_fusion.2.field, bf16[64,576]{1,0:T(8,128)(2,1)S(1)} %bitcast.61), custom_call_target="tpu_custom_call" | custom-call | flops 603979776 | bytes 3342336 | tf_op jit(solution)/shard_map/pallas_call | solution.py:90
  209.6 7.3 %collective-permute-start.12 = (bf16[8,64,256]{2,1,0:T(8,128)(2,1)S(1)}, bf16[8,64,256]{2,1,0:T(8,128)(2,1)S(1)}, u32[]{:S(2)}, u32[]{:S(2)}) collective-permute-start(bf16[8,64,256]{2,1,0:T(8,128)(2,1)S(1)} %get-tuple-element.44), channel_id=1, source_target_pairs={{0,2},{2,4},{4,6},{6,8},{8,10},{10,12},{12,14},{14,16},{16,18},{18... | collective-permute-start | bytes 786440 | tf_op jit(solution)/shard_map/ppermute | solution.py:22
  219.2 9.6 %collective-permute-done.13 = bf16[8,64,256]{2,1,0:T(8,128)(2,1)S(1)} collective-permute-done((bf16[8,64,256]{2,1,0:T(8,128)(2,1)S(1)}, bf16[8,64,256]{2,1,0:T(8,128)(2,1)S(1)}, u32[]{:S(2)}, u32[]{:S(2)}) %collective-permute-start.13) | collective-permute-done | bytes 262176 | tf_op jit(solution)/shard_map/ppermute | solution.py:24
  235.9 5.8 %collective-permute-start.14 = (bf16[48,64,8]{1,2,0:T(8,128)(2,1)}, bf16[48,64,8]{1,2,0:T(8,128)(2,1)}, u32[]{:S(2)}, u32[]{:S(2)}) collective-permute-start(bf16[48,64,8]{1,2,0:T(8,128)(2,1)} %copy.66), channel_id=1, source_target_pairs={{0,1},{2,3},{4,5},{6,7},{8,9},{10,11},{12,13},{14,15},{16,17},{18,... | collective-permute-start | bytes 147464 | tf_op jit(solution)/shard_map/ppermute | solution.py:22
  241.7 12.0 %shard_map.149 = f32[576,64]{1,0:T(8,128)S(1)} custom-call(bf16[48,64,272]{2,1,0:T(8,128)(2,1)S(1)} %pad_maximum_fusion.field, bf16[32,64,256]{2,1,0:T(8,128)(2,1)S(1)} %get-tuple-element.33.grad), custom_call_target="tpu_custom_call" | custom-call | flops 603979776 | bytes 3342336 | tf_op jit(solution)/shard_map/pallas_call | solution.py:90
  256.2 2.1 copy.68
  260.3 3.3 %pad_maximum_fusion.3.field = bf16[48,64,272]{2,1,0:T(8,128)(2,1)S(1)} fusion(bf16[48,64,8]{2,1,0:T(8,128)(2,1)} %copy.69, bf16[8,64,256]{2,1,0:T(8,128)(2,1)} %copy-done.24, bf16[32,64,256]{2,1,0:T(8,128)(2,1)S(1)} %get-tuple-element.33.grad, bf16[8,64,256]{2,1,0:T(8,128)(2,1)} %copy-done.23, bf16[48,64,8]{2,1,0:T(8,128)(2,1)} %copy.68), kind=kLoop, calls=%fused_computation.8 | loop fusion | flops 8355840 | bytes 3342336 | tf_op jit(solution)/shard_map/concatenate | solution.py:20
  263.7 10.8 %shard_map.148 = f32[32,64,256]{2,1,0:T(8,128)S(1)} custom-call(bf16[48,64,272]{2,1,0:T(8,128)(2,1)S(1)} %pad_maximum_fusion.3.field, bf16[64,576]{1,0:T(8,128)(2,1)S(1)} %bitcast.60), custom_call_target="tpu_custom_call" | custom-call | flops 603979776 | bytes 3342336 | tf_op jit(solution)/shard_map/pallas_call | solution.py:90
  277.8 29.0 %shard_map.151 = f32[16,40,128]{2,1,0:T(8,128)} custom-call(f32[16,40,128]{2,1,0:T(8,128)} %bitcast.70), custom_call_target="tpu_custom_call" | custom-call | tf_op jit(solution)/shard_map/pallas_call | solution.py:313
  (173 shorter events, 87.0 us)
Async XLA Ops:
  0.6 123.3 %copy-start = (bf16[64,37]{0,1:T(8,128)(2,1)S(1)}, bf16[64,37]{0,1:T(8,128)(2,1)}, u32[]{:S(2)}) copy-start(bf16[64,37]{0,1:T(8,128)(2,1)} %param.14) | copy-start | bytes 14212
  2.6 5.0 %collective-permute-start = (bf16[8,64,256]{2,1,0:T(8,128)(2,1)S(1)}, bf16[8,64,256]{2,1,0:T(8,128)(2,1)S(1)}, u32[]{:S(2)}, u32[]{:S(2)}) collective-permute-start(bf16[8,64,256]{2,1,0:T(8,128)(2,1)S(1)} %get-tuple-element.54), channel_id=1, source_target_pairs={{0,2},{2,4},{4,6},{6,8},{8,10},{10,12},{12,14},{14,16},{16,18},{18... | collective-permute-start | bytes 786440 | tf_op jit(solution)/shard_map/ppermute | solution.py:22
  5.0 5.5 %collective-permute-start.1 = (bf16[8,64,256]{2,1,0:T(8,128)(2,1)S(1)}, bf16[8,64,256]{2,1,0:T(8,128)(2,1)S(1)}, u32[]{:S(2)}, u32[]{:S(2)}) collective-permute-start(bf16[8,64,256]{2,1,0:T(8,128)(2,1)S(1)} %get-tuple-element.55), channel_id=1, source_target_pairs={{2,0},{4,2},{6,4},{8,6},{10,8},{12,10},{14,12},{16,14},{18,16},{20... | collective-permute-start | bytes 786440 | tf_op jit(solution)/shard_map/ppermute | solution.py:24
  14.4 9.3 %collective-permute-start.3 = (bf16[48,64,8]{1,2,0:T(8,128)(2,1)S(1)}, bf16[48,64,8]{1,2,0:T(8,128)(2,1)S(1)}, u32[]{:S(2)}, u32[]{:S(2)}) collective-permute-start(bf16[48,64,8]{1,2,0:T(8,128)(2,1)S(1)} %copy.44), channel_id=1, source_target_pairs={{1,0},{3,2},{5,4},{7,6},{9,8},{11,10},{13,12},{15,14},{17,16},{19,... | collective-permute-start | bytes 147464 | tf_op jit(solution)/shard_map/ppermute | solution.py:24
  15.7 6.8 %collective-permute-start.2 = (bf16[48,64,8]{1,2,0:T(8,128)(2,1)S(1)}, bf16[48,64,8]{1,2,0:T(8,128)(2,1)S(1)}, u32[]{:S(2)}, u32[]{:S(2)}) collective-permute-start(bf16[48,64,8]{1,2,0:T(8,128)(2,1)S(1)} %copy.43), channel_id=1, source_target_pairs={{0,1},{2,3},{4,5},{6,7},{8,9},{10,11},{12,13},{14,15},{16,17},{18,... | collective-permute-start | bytes 147464 | tf_op jit(solution)/shard_map/ppermute | solution.py:22
  28.2 10.8 %copy-start.39 = (f32[64]{0:T(128)S(1)}, f32[64]{0:T(128)}, u32[]{:S(2)}) copy-start(f32[64]{0:T(128)} %param.11) | copy-start | bytes 772
  40.4 7.0 %collective-permute-start.4 = (bf16[8,64,256]{2,1,0:T(8,128)(2,1)S(1)}, bf16[8,64,256]{2,1,0:T(8,128)(2,1)S(1)}, u32[]{:S(2)}, u32[]{:S(2)}) collective-permute-start(bf16[8,64,256]{2,1,0:T(8,128)(2,1)S(1)} %get-tuple-element.52), channel_id=1, source_target_pairs={{0,2},{2,4},{4,6},{6,8},{8,10},{10,12},{12,14},{14,16},{16,18},{18... | collective-permute-start | bytes 786440 | tf_op jit(solution)/shard_map/ppermute | solution.py:22
  45.9 3.9 %collective-permute-start.5 = (bf16[8,64,256]{2,1,0:T(8,128)(2,1)S(1)}, bf16[8,64,256]{2,1,0:T(8,128)(2,1)S(1)}, u32[]{:S(2)}, u32[]{:S(2)}) collective-permute-start(bf16[8,64,256]{2,1,0:T(8,128)(2,1)S(1)} %get-tuple-element.53), channel_id=1, source_target_pairs={{2,0},{4,2},{6,4},{8,6},{10,8},{12,10},{14,12},{16,14},{18,16},{20... | collective-permute-start | bytes 786440 | tf_op jit(solution)/shard_map/ppermute | solution.py:24
  50.0 12.1 %copy-start.35 = (s32[32,256]{1,0:T(8,128)S(1)}, s32[32,256]{1,0:T(8,128)}, u32[]{:S(2)}) copy-start(s32[32,256]{1,0:T(8,128)} %param.16) | copy-start | bytes 98308
  50.0 12.9 %copy-start.27 = (bf16[3,3,64,64]{3,2,1,0:T(8,128)(2,1)S(1)}, bf16[3,3,64,64]{3,2,1,0:T(8,128)(2,1)}, u32[]{:S(2)}) copy-start(bf16[3,3,64,64]{3,2,1,0:T(8,128)(2,1)} %param.12) | copy-start | bytes 221188
  51.4 12.9 %copy-start.28 = (bf16[3,3,64,64]{2,3,1,0:T(8,128)(2,1)S(1)}, bf16[3,3,64,64]{2,3,1,0:T(8,128)(2,1)}, u32[]{:S(2)}) copy-start(bf16[3,3,64,64]{2,3,1,0:T(8,128)(2,1)} %reverse_bitcast_fusion.1) | copy-start | bytes 221188
  54.4 12.1 %collective-permute-start.7 = (bf16[48,64,8]{1,2,0:T(8,128)(2,1)}, bf16[48,64,8]{1,2,0:T(8,128)(2,1)}, u32[]{:S(2)}, u32[]{:S(2)}) collective-permute-start(bf16[48,64,8]{1,2,0:T(8,128)(2,1)} %copy.49), channel_id=1, source_target_pairs={{1,0},{3,2},{5,4},{7,6},{9,8},{11,10},{13,12},{15,14},{17,16},{19,... | collective-permute-start | bytes 147464 | tf_op jit(solution)/shard_map/ppermute | solution.py:24
  55.7 9.6 %collective-permute-start.6 = (bf16[48,64,8]{1,2,0:T(8,128)(2,1)}, bf16[48,64,8]{1,2,0:T(8,128)(2,1)}, u32[]{:S(2)}, u32[]{:S(2)}) collective-permute-start(bf16[48,64,8]{1,2,0:T(8,128)(2,1)} %copy.48), channel_id=1, source_target_pairs={{0,1},{2,3},{4,5},{6,7},{8,9},{10,11},{12,13},{14,15},{16,17},{18,... | collective-permute-start | bytes 147464 | tf_op jit(solution)/shard_map/ppermute | solution.py:22
  71.9 10.8 %copy-start.2 = (bf16[48,64,272]{2,1,0:T(8,128)(2,1)}, bf16[48,64,272]{2,1,0:T(8,128)(2,1)S(1)}, u32[]{:S(2)}) copy-start(bf16[48,64,272]{2,1,0:T(8,128)(2,1)S(1)} %pad_maximum_fusion.1.field) | copy-start | bytes 5013508
  71.9 10.8 %copy-start.17 = (bf16[64,32,256]{2,1,0:T(8,128)(2,1)S(1)}, bf16[64,32,256]{2,1,0:T(8,128)(2,1)}, u32[]{:S(2)}) copy-start(bf16[64,32,256]{2,1,0:T(8,128)(2,1)} %param.9) | copy-start | bytes 3145732
  72.0 10.8 %copy-start.41 = (f32[64]{0:T(128)S(1)}, f32[64]{0:T(128)}, u32[]{:S(2)}) copy-start(f32[64]{0:T(128)} %param.13) | copy-start | bytes 772
  84.2 42.2 %copy-start.13 = (bf16[32,64,256]{2,1,0:T(8,128)(2,1)}, bf16[32,64,256]{2,1,0:T(8,128)(2,1)S(1)}, u32[]{:S(2)}) copy-start(bf16[32,64,256]{2,1,0:T(8,128)(2,1)S(1)} %fusion.4) | copy-start | bytes 3145732
  130.0 14.9 %copy-start.14 = (bf16[32,64,256]{2,1,0:T(8,128)(2,1)S(1)}, bf16[32,64,256]{2,1,0:T(8,128)(2,1)}, u32[]{:S(2)}) copy-start(bf16[32,64,256]{2,1,0:T(8,128)(2,1)} %copy-done.13) | copy-start | bytes 3145732
  130.0 14.9 %copy-start.15 = (f32[32,37,256]{2,1,0:T(8,128)S(1)}, f32[32,37,256]{2,1,0:T(8,128)}, u32[]{:S(2)}) copy-start(f32[32,37,256]{2,1,0:T(8,128)} %get-tuple-element.61) | copy-start | bytes 3637252
  130.0 14.9 %copy-start.31 = (f32[32,256]{1,0:T(8,128)S(1)}, f32[32,256]{1,0:T(8,128)}, u32[]{:S(2)}) copy-start(f32[32,256]{1,0:T(8,128)} %get-tuple-element.60) | copy-start | bytes 98308
  130.0 14.9 %copy-start.33 = (s32[32,256]{1,0:T(8,128)S(1)}, s32[32,256]{1,0:T(8,128)}, u32[]{:S(2)}) copy-start(s32[32,256]{1,0:T(8,128)} %reshape.115) | copy-start | bytes 98308
  130.0 14.9 %copy-start.36 = (s32[32,256]{1,0:T(8,128)S(1)}, s32[32,256]{1,0:T(8,128)}, u32[]{:S(2)}) copy-start(s32[32,256]{1,0:T(8,128)} %param.16) | copy-start | bytes 98308
  138.2 9.7 %collective-permute-start.8 = (bf16[8,64,256]{2,1,0:T(8,128)(2,1)}, bf16[8,64,256]{2,1,0:T(8,128)(2,1)}, u32[]{:S(2)}, u32[]{:S(2)}) collective-permute-start(bf16[8,64,256]{2,1,0:T(8,128)(2,1)} %get-tuple-element.46), channel_id=1, source_target_pairs={{0,2},{2,4},{4,6},{6,8},{8,10},{10,12},{12,14},{14,16},{16,18},{18... | collective-permute-start | bytes 786440 | tf_op jit(solution)/shard_map/ppermute | solution.py:22
  143.5 7.0 %collective-permute-start.9 = (bf16[8,64,256]{2,1,0:T(8,128)(2,1)}, bf16[8,64,256]{2,1,0:T(8,128)(2,1)}, u32[]{:S(2)}, u32[]{:S(2)}) collective-permute-start(bf16[8,64,256]{2,1,0:T(8,128)(2,1)} %get-tuple-element.47), channel_id=1, source_target_pairs={{2,0},{4,2},{6,4},{8,6},{10,8},{12,10},{14,12},{16,14},{18,16},{20... | collective-permute-start | bytes 786440 | tf_op jit(solution)/shard_map/ppermute | solution.py:24
  157.3 35.1 %collective-permute-start.11 = (bf16[48,64,8]{1,2,0:T(8,128)(2,1)}, bf16[48,64,8]{1,2,0:T(8,128)(2,1)}, u32[]{:S(2)}, u32[]{:S(2)}) collective-permute-start(bf16[48,64,8]{1,2,0:T(8,128)(2,1)} %copy.61), channel_id=1, source_target_pairs={{1,0},{3,2},{5,4},{7,6},{9,8},{11,10},{13,12},{15,14},{17,16},{19,... | collective-permute-start | bytes 147464 | tf_op jit(solution)/shard_map/ppermute | solution.py:24
  158.6 31.8 %collective-permute-start.10 = (bf16[48,64,8]{1,2,0:T(8,128)(2,1)}, bf16[48,64,8]{1,2,0:T(8,128)(2,1)}, u32[]{:S(2)}, u32[]{:S(2)}) collective-permute-start(bf16[48,64,8]{1,2,0:T(8,128)(2,1)} %copy.60), channel_id=1, source_target_pairs={{0,1},{2,3},{4,5},{6,7},{8,9},{10,11},{12,13},{14,15},{16,17},{18,... | collective-permute-start | bytes 147464 | tf_op jit(solution)/shard_map/ppermute | solution.py:22
  209.6 9.6 %collective-permute-start.12 = (bf16[8,64,256]{2,1,0:T(8,128)(2,1)S(1)}, bf16[8,64,256]{2,1,0:T(8,128)(2,1)S(1)}, u32[]{:S(2)}, u32[]{:S(2)}) collective-permute-start(bf16[8,64,256]{2,1,0:T(8,128)(2,1)S(1)} %get-tuple-element.44), channel_id=1, source_target_pairs={{0,2},{2,4},{4,6},{6,8},{8,10},{10,12},{12,14},{14,16},{16,18},{18... | collective-permute-start | bytes 786440 | tf_op jit(solution)/shard_map/ppermute | solution.py:22
  216.9 11.9 %collective-permute-start.13 = (bf16[8,64,256]{2,1,0:T(8,128)(2,1)S(1)}, bf16[8,64,256]{2,1,0:T(8,128)(2,1)S(1)}, u32[]{:S(2)}, u32[]{:S(2)}) collective-permute-start(bf16[8,64,256]{2,1,0:T(8,128)(2,1)S(1)} %get-tuple-element.45), channel_id=1, source_target_pairs={{2,0},{4,2},{6,4},{8,6},{10,8},{12,10},{14,12},{16,14},{18,16},{20... | collective-permute-start | bytes 786440 | tf_op jit(solution)/shard_map/ppermute | solution.py:24
  219.2 11.4 %copy-start.23 = (bf16[8,64,256]{2,1,0:T(8,128)(2,1)}, bf16[8,64,256]{2,1,0:T(8,128)(2,1)S(1)}, u32[]{:S(2)}) copy-start(bf16[8,64,256]{2,1,0:T(8,128)(2,1)S(1)} %collective-permute-done.12) | copy-start | bytes 786436
  234.6 23.7 %collective-permute-start.15 = (bf16[48,64,8]{1,2,0:T(8,128)(2,1)}, bf16[48,64,8]{1,2,0:T(8,128)(2,1)}, u32[]{:S(2)}, u32[]{:S(2)}) collective-permute-start(bf16[48,64,8]{1,2,0:T(8,128)(2,1)} %copy.67), channel_id=1, source_target_pairs={{1,0},{3,2},{5,4},{7,6},{9,8},{11,10},{13,12},{15,14},{17,16},{19,... | collective-permute-start | bytes 147464 | tf_op jit(solution)/shard_map/ppermute | solution.py:24
  235.9 20.3 %collective-permute-start.14 = (bf16[48,64,8]{1,2,0:T(8,128)(2,1)}, bf16[48,64,8]{1,2,0:T(8,128)(2,1)}, u32[]{:S(2)}, u32[]{:S(2)}) collective-permute-start(bf16[48,64,8]{1,2,0:T(8,128)(2,1)} %copy.66), channel_id=1, source_target_pairs={{0,1},{2,3},{4,5},{6,7},{8,9},{10,11},{12,13},{14,15},{16,17},{18,... | collective-permute-start | bytes 147464 | tf_op jit(solution)/shard_map/ppermute | solution.py:22
  277.8 39.8 %copy-start.1 = (bf16[64,37]{0,1:T(8,128)(2,1)S(1)}, bf16[64,37]{0,1:T(8,128)(2,1)}, u32[]{:S(2)}) copy-start(bf16[64,37]{0,1:T(8,128)(2,1)} %param.14) | copy-start | bytes 14212
  (26 other events, 123.5 us)

commit v4 on v3

--- a/solution.py
+++ b/solution.py
@@ -44,7 +44,7 @@
     rows, _, cols = shifted.shape
     chans = field.shape[1]
 
-    @pl.loop(0, rows)
+    @pl.loop(0, rows, unroll=4)
     def _(row):
         line = field[row]
         for tap in range(KERNEL_TAPS):
@@ -61,7 +61,7 @@
 def conv_kernel(field, weight, out, shifted):
     spread_taps(field, shifted)
 
-    @pl.loop(0, out.shape[0])
+    @pl.loop(0, out.shape[0], unroll=4)
     def _(row):
         out[row] = jnp.dot(
             weight[...], tap_stack(shifted, row), preferred_element_type=jnp.float32
@@ -72,7 +72,7 @@
     spread_taps(field, shifted)
     out[...] = jnp.zeros_like(out)
 
-    @pl.loop(0, grad.shape[0])
+    @pl.loop(0, grad.shape[0], unroll=4)
     def _(row):
         out[...] += lax.dot_general(
             tap_stack(shifted, row),

time: 321 us -> 288 us (0.90)
  Pallas kernels: 123 us -> 90.3 us
    pallas_call x6, Pallas kernels: 67.3 us -> 34.7 us  [row_call(): pl.pallas_call(kernel, out_shape=jax.ShapeDtypeStruct(out_shape, jnp.floa...]
  transfers between devices with their start and end apart: 16 -> 16, of which waited for: 5 -> 5; matrix products, arithmetic and copies ran while one was open for 6% -> 7% of each run, Pallas kernels for 8% -> 5%
where the time goes in v4:
time: 288 us; the launch traced here: 285 us
  Pallas kernels  90.3 us (31%)
  local copies, waits for them, and re-layouts  67.2 us (23%)
  starting transfers between devices  62.9 us (22%)
  other arithmetic  30.3 us (11%)
  waiting for transfers between devices  18.6 us (6%)
  matrix products  14.4 us (5%)
    ppermute x8, starting transfers between devices, with_halo(): lax.ppermute(tail, axis, [(i, (i + 1) % count) for i in range(ends)])  52.3 us
    pallas_call x6, Pallas kernels, row_call(): pl.pallas_call(kernel, out_shape=jax.ShapeDtypeStruct(out_shape, jnp.floa...  34.7 us
    pallas_call x1, Pallas kernels, summed_over_mesh(): pl.pallas_call(functools.partial(sum_kernel, row_axis, column_axis), out_...  29 us
    pallas_call x1, Pallas kernels, swapped(): pl.pallas_call(functools.partial(swap_kernel, count), out_shape=[jax.Shap...  26.6 us
    ppermute x8, waiting for transfers between devices, with_halo(): lax.ppermute(head, axis, [((i + 1) % count, i) for i in range(ends)])  17.5 us
    concatenate x8, other arithmetic, with_halo(): jnp.concatenate([lax.ppermute(tail, axis, [(i, (i + 1) % count) for i in...  15.2 us
    slice x12, local copies, waits for them, and re-layouts, with_halo(): lax.slice_in_dim(cells, cells.shape[dim] - width, cells.shape[dim], axis=...  14.2 us
    ppermute x8, starting transfers between devices, with_halo(): lax.ppermute(head, axis, [((i + 1) % count, i) for i in range(ends)])  10.6 us
  transfers between devices with their start and end apart: 16, of which 5 were waited for; matrix products, arithmetic and copies ran while one was open for 7% of the time, Pallas kernels for 5%

profile of v4, /device:TPU:0, one launch (start us, length us, event | category | flops | bytes accessed | tf_op | source)
XLA Modules:
  0.0 285.1 jit_solution(622207558865751248)
XLA Ops:
  2.6 2.4 collective-permute-start
  7.6 2.9 %collective-permute-done.1 = bf16[8,64,256]{2,1,0:T(8,128)(2,1)S(1)} collective-permute-done((bf16[8,64,256]{2,1,0:T(8,128)(2,1)S(1)}, bf16[8,64,256]{2,1,0:T(8,128)(2,1)S(1)}, u32[]{:S(2)}, u32[]{:S(2)}) %collective-permute-start.1) | collective-permute-done | bytes 262176 | tf_op jit(solution)/shard_map/ppermute | solution.py:24
  15.7 4.6 %collective-permute-start.2 = (bf16[48,64,8]{1,2,0:T(8,128)(2,1)S(1)}, bf16[48,64,8]{1,2,0:T(8,128)(2,1)S(1)}, u32[]{:S(2)}, u32[]{:S(2)}) collective-permute-start(bf16[48,64,8]{1,2,0:T(8,128)(2,1)S(1)} %copy.43), channel_id=1, source_target_pairs={{0,1},{2,3},{4,5},{6,7},{8,9},{10,11},{12,13},{14,15},{16,17},{18,... | collective-permute-start | bytes 147464 | tf_op jit(solution)/shard_map/ppermute | solution.py:22
  24.9 3.3 %pad_maximum_fusion.field = bf16[48,64,272]{2,1,0:T(8,128)(2,1)S(1)} fusion(bf16[48,64,8]{2,1,0:T(8,128)(2,1)} %copy.46, bf16[8,64,256]{2,1,0:T(8,128)(2,1)} %copy-done.20, bf16[32,64,256]{2,1,0:T(8,128)(2,1)S(1)} %bitcast.66, bf16[8,64,256]{2,1,0:T(8,128)(2,1)} %copy-done.19, bf16[48,64,8]{2,1,0:T(8,128)(2,1)} %copy.45), kind=kLoop, calls=%fused_computation.5 | loop fusion | flops 8355840 | bytes 3342336 | tf_op jit(solution)/shard_map/concatenate | solution.py:20
  28.2 5.2 %shard_map.144 = f32[32,64,256]{2,1,0:T(8,128)S(1)} custom-call(bf16[48,64,272]{2,1,0:T(8,128)(2,1)S(1)} %pad_maximum_fusion.field, bf16[64,576]{1,0:T(8,128)(2,1)S(1)} %bitcast.63), custom_call_target="tpu_custom_call" | custom-call | flops 603979776 | bytes 3342336 | tf_op jit(solution)/shard_map/pallas_call | solution.py:90
  34.8 5.5 %collective-permute-start.4 = (bf16[8,64,256]{2,1,0:T(8,128)(2,1)S(1)}, bf16[8,64,256]{2,1,0:T(8,128)(2,1)S(1)}, u32[]{:S(2)}, u32[]{:S(2)}) collective-permute-start(bf16[8,64,256]{2,1,0:T(8,128)(2,1)S(1)} %get-tuple-element.52), channel_id=1, source_target_pairs={{0,2},{2,4},{4,6},{6,8},{8,10},{10,12},{12,14},{14,16},{16,18},{18... | collective-permute-start | bytes 786440 | tf_op jit(solution)/shard_map/ppermute | solution.py:22
  41.8 2.4 collective-permute-done.5
  45.8 2.1 copy.48
  50.1 5.8 %collective-permute-start.6 = (bf16[48,64,8]{1,2,0:T(8,128)(2,1)}, bf16[48,64,8]{1,2,0:T(8,128)(2,1)}, u32[]{:S(2)}, u32[]{:S(2)}) collective-permute-start(bf16[48,64,8]{1,2,0:T(8,128)(2,1)} %copy.48), channel_id=1, source_target_pairs={{0,1},{2,3},{4,5},{6,7},{8,9},{10,11},{12,13},{14,15},{16,17},{18,... | collective-permute-start | bytes 147464 | tf_op jit(solution)/shard_map/ppermute | solution.py:22
  60.9 2.1 copy.51
  63.0 3.3 %pad_maximum_fusion.1.field = bf16[48,64,272]{2,1,0:T(8,128)(2,1)S(1)} fusion(bf16[48,64,8]{2,1,0:T(8,128)(2,1)} %copy.51, bf16[8,64,256]{2,1,0:T(8,128)(2,1)} %copy-done.22, bf16[32,64,256]{2,1,0:T(8,128)(2,1)} %copy-done.12, bf16[8,64,256]{2,1,0:T(8,128)(2,1)} %copy-done.21, bf16[48,64,8]{2,1,0:T(8,128)(2,1)S(1)} %copy.50), kind=kLoop, calls=%fused_computation.6 | loop fusion | flops 8355840 | bytes 3342336 | tf_op jit(solution)/shard_map/concatenate | solution.py:20
  66.4 5.2 %shard_map.145 = f32[32,64,256]{2,1,0:T(8,128)S(1)} custom-call(bf16[48,64,272]{2,1,0:T(8,128)(2,1)S(1)} %pad_maximum_fusion.1.field, bf16[64,576]{1,0:T(8,128)(2,1)S(1)} %bitcast.62), custom_call_target="tpu_custom_call" | custom-call | flops 603979776 | bytes 3342336 | tf_op jit(solution)/shard_map/pallas_call | solution.py:90
  74.3 2.6 copy.77
  77.0 26.6 %shard_map.146 = (bf16[8,512,128]{2,1,0:T(8,128)(2,1)}, bf16[8,8,128]{2,1,0:T(8,128)(2,1)}) custom-call(bf16[8,512,128]{2,1,0:T(8,128)(2,1)} %bitcast.69, bf16[8,8,128]{2,1,0:T(8,128)(2,1)} %reshape.107.small_src), custom_call_target="tpu_custom_call" | custom-call | tf_op jit(solution)/shard_map/pallas_call | solution.py:203
  112.8 2.4 fusion.13
  115.2 3.6 %fusion.30 = (f32[32,256]{1,0:T(8,128)}, f32[32,37,256]{2,1,0:T(8,128)}) fusion(f32[32,256,37]{1,2,0:T(8,128)} %fusion.13, bf16[32,64,256]{2,1,0:T(8,128)(2,1)S(1)} %fusion.4, f32[37]{0:T(128)S(1)} %copy-done.40, bf16[64,37]{0,1:T(8,128)(2,1)S(1)} %copy-done), kind=kOutput, calls=%fused_computation.65 | convolution fusion | flops 40312868 | bytes 3511060 | tf_op jit(solution)/shard_map/sub | solution.py:373
  118.8 6.3 %fusion.31 = (bf16[32,64,256]{2,1,0:T(8,128)(2,1)S(1)}, f32[32,64,256]{2,1,0:T(8,128)}) fusion(f32[32,64,256]{2,1,0:T(8,128)} %copy-done.8, f32[64]{0:T(128)S(1)} %copy-done.41, bf16[64,32,256]{2,1,0:T(8,128)(2,1)} %param.9, f32[32,256]{1,0:T(8,128)S(1)} %broadcast_multiply_fusion, bf16[64,37]{0,1:T(8,128)(2,1)S(1)} %copy-done, ...), kind=kOutput, calls=%fused_computation.66 | convolution fusion | flops 240230400 | bytes 7639936 | tf_op jit(solution)/shard_map/ck,ikj->icj/dot_general | solution.py:387
  127.0 5.3 %collective-permute-start.8 = (bf16[8,64,256]{2,1,0:T(8,128)(2,1)}, bf16[8,64,256]{2,1,0:T(8,128)(2,1)}, u32[]{:S(2)}, u32[]{:S(2)}) collective-permute-start(bf16[8,64,256]{2,1,0:T(8,128)(2,1)} %get-tuple-element.46), channel_id=1, source_target_pairs={{0,2},{2,4},{4,6},{6,8},{8,10},{10,12},{12,14},{14,16},{16,18},{18... | collective-permute-start | bytes 786440 | tf_op jit(solution)/shard_map/ppermute | solution.py:22
  136.7 2.6 collective-permute-done.9
  147.4 15.6 %collective-permute-start.10 = (bf16[48,64,8]{1,2,0:T(8,128)(2,1)}, bf16[48,64,8]{1,2,0:T(8,128)(2,1)}, u32[]{:S(2)}, u32[]{:S(2)}) collective-permute-start(bf16[48,64,8]{1,2,0:T(8,128)(2,1)} %copy.60), channel_id=1, source_target_pairs={{0,1},{2,3},{4,5},{6,7},{8,9},{10,11},{12,13},{14,15},{16,17},{18,... | collective-permute-start | bytes 147464 | tf_op jit(solution)/shard_map/ppermute | solution.py:22
  164.7 7.0 %shard_map.150 = f32[576,64]{1,0:T(8,128)S(1)} custom-call(bf16[48,64,272]{2,1,0:T(8,128)(2,1)S(1)} %copy-done.3, bf16[32,64,256]{2,1,0:T(8,128)(2,1)S(1)} %copy-done.7), custom_call_target="tpu_custom_call" | custom-call | flops 603979776 | bytes 3342336 | tf_op jit(solution)/shard_map/pallas_call | solution.py:90
  178.2 3.4 %pad_maximum_fusion.2.field = bf16[48,64,272]{2,1,0:T(8,128)(2,1)S(1)} fusion(bf16[48,64,8]{2,1,0:T(8,128)(2,1)} %copy.63, bf16[8,64,256]{2,1,0:T(8,128)(2,1)} %collective-permute-done.9, bf16[32,64,256]{2,1,0:T(8,128)(2,1)S(1)} %copy-done.7, bf16[8,64,256]{2,1,0:T(8,128)(2,1)} %collective-permute-done.8, bf16[48,64,8]{2,1,0:T(8,128)(2,1)} %copy.62), kind=kLoop, calls=%fused_computation.7 | loop fusion | flops 8355840 | bytes 3342336 | tf_op jit(solution)/shard_map/concatenate | solution.py:20
  181.6 5.2 %shard_map.147 = f32[32,64,256]{2,1,0:T(8,128)S(1)} custom-call(bf16[48,64,272]{2,1,0:T(8,128)(2,1)S(1)} %pad_maximum_fusion.2.field, bf16[64,576]{1,0:T(8,128)(2,1)S(1)} %bitcast.61), custom_call_target="tpu_custom_call" | custom-call | flops 603979776 | bytes 3342336 | tf_op jit(solution)/shard_map/pallas_call | solution.py:90
  187.7 7.3 %collective-permute-start.12 = (bf16[8,64,256]{2,1,0:T(8,128)(2,1)S(1)}, bf16[8,64,256]{2,1,0:T(8,128)(2,1)S(1)}, u32[]{:S(2)}, u32[]{:S(2)}) collective-permute-start(bf16[8,64,256]{2,1,0:T(8,128)(2,1)S(1)} %get-tuple-element.44), channel_id=1, source_target_pairs={{0,2},{2,4},{4,6},{6,8},{8,10},{10,12},{12,14},{14,16},{16,18},{18... | collective-permute-start | bytes 786440 | tf_op jit(solution)/shard_map/ppermute | solution.py:22
  197.3 9.6 %collective-permute-done.13 = bf16[8,64,256]{2,1,0:T(8,128)(2,1)S(1)} collective-permute-done((bf16[8,64,256]{2,1,0:T(8,128)(2,1)S(1)}, bf16[8,64,256]{2,1,0:T(8,128)(2,1)S(1)}, u32[]{:S(2)}, u32[]{:S(2)}) %collective-permute-start.13) | collective-permute-done | bytes 262176 | tf_op jit(solution)/shard_map/ppermute | solution.py:24
  214.0 5.8 %collective-permute-start.14 = (bf16[48,64,8]{1,2,0:T(8,128)(2,1)}, bf16[48,64,8]{1,2,0:T(8,128)(2,1)}, u32[]{:S(2)}, u32[]{:S(2)}) collective-permute-start(bf16[48,64,8]{1,2,0:T(8,128)(2,1)} %copy.66), channel_id=1, source_target_pairs={{0,1},{2,3},{4,5},{6,7},{8,9},{10,11},{12,13},{14,15},{16,17},{18,... | collective-permute-start | bytes 147464 | tf_op jit(solution)/shard_map/ppermute | solution.py:22
  219.9 7.0 %shard_map.149 = f32[576,64]{1,0:T(8,128)S(1)} custom-call(bf16[48,64,272]{2,1,0:T(8,128)(2,1)S(1)} %pad_maximum_fusion.field, bf16[32,64,256]{2,1,0:T(8,128)(2,1)S(1)} %get-tuple-element.33.grad), custom_call_target="tpu_custom_call" | custom-call | flops 603979776 | bytes 3342336 | tf_op jit(solution)/shard_map/pallas_call | solution.py:90
  229.3 2.1 copy.68
  231.4 2.1 copy.69
  233.4 3.3 %pad_maximum_fusion.3.field = bf16[48,64,272]{2,1,0:T(8,128)(2,1)S(1)} fusion(bf16[48,64,8]{2,1,0:T(8,128)(2,1)} %copy.69, bf16[8,64,256]{2,1,0:T(8,128)(2,1)} %copy-done.24, bf16[32,64,256]{2,1,0:T(8,128)(2,1)S(1)} %get-tuple-element.33.grad, bf16[8,64,256]{2,1,0:T(8,128)(2,1)} %copy-done.23, bf16[48,64,8]{2,1,0:T(8,128)(2,1)} %copy.68), kind=kLoop, calls=%fused_computation.8 | loop fusion | flops 8355840 | bytes 3342336 | tf_op jit(solution)/shard_map/concatenate | solution.py:20
  236.8 5.2 %shard_map.148 = f32[32,64,256]{2,1,0:T(8,128)S(1)} custom-call(bf16[48,64,272]{2,1,0:T(8,128)(2,1)S(1)} %pad_maximum_fusion.3.field, bf16[64,576]{1,0:T(8,128)(2,1)S(1)} %bitcast.60), custom_call_target="tpu_custom_call" | custom-call | flops 603979776 | bytes 3342336 | tf_op jit(solution)/shard_map/pallas_call | solution.py:90
  245.3 29.0 %shard_map.151 = f32[16,40,128]{2,1,0:T(8,128)} custom-call(f32[16,40,128]{2,1,0:T(8,128)} %bitcast.70), custom_call_target="tpu_custom_call" | custom-call | tf_op jit(solution)/shard_map/pallas_call | solution.py:313
  (173 shorter events, 87.0 us)
Async XLA Ops:
  0.6 112.1 %copy-start = (bf16[64,37]{0,1:T(8,128)(2,1)S(1)}, bf16[64,37]{0,1:T(8,128)(2,1)}, u32[]{:S(2)}) copy-start(bf16[64,37]{0,1:T(8,128)(2,1)} %param.14) | copy-start | bytes 14212
  2.6 5.0 %collective-permute-start = (bf16[8,64,256]{2,1,0:T(8,128)(2,1)S(1)}, bf16[8,64,256]{2,1,0:T(8,128)(2,1)S(1)}, u32[]{:S(2)}, u32[]{:S(2)}) collective-permute-start(bf16[8,64,256]{2,1,0:T(8,128)(2,1)S(1)} %get-tuple-element.54), channel_id=1, source_target_pairs={{0,2},{2,4},{4,6},{6,8},{8,10},{10,12},{12,14},{14,16},{16,18},{18... | collective-permute-start | bytes 786440 | tf_op jit(solution)/shard_map/ppermute | solution.py:22
  5.0 5.5 %collective-permute-start.1 = (bf16[8,64,256]{2,1,0:T(8,128)(2,1)S(1)}, bf16[8,64,256]{2,1,0:T(8,128)(2,1)S(1)}, u32[]{:S(2)}, u32[]{:S(2)}) collective-permute-start(bf16[8,64,256]{2,1,0:T(8,128)(2,1)S(1)} %get-tuple-element.55), channel_id=1, source_target_pairs={{2,0},{4,2},{6,4},{8,6},{10,8},{12,10},{14,12},{16,14},{18,16},{20... | collective-permute-start | bytes 786440 | tf_op jit(solution)/shard_map/ppermute | solution.py:24
  14.4 9.3 %collective-permute-start.3 = (bf16[48,64,8]{1,2,0:T(8,128)(2,1)S(1)}, bf16[48,64,8]{1,2,0:T(8,128)(2,1)S(1)}, u32[]{:S(2)}, u32[]{:S(2)}) collective-permute-start(bf16[48,64,8]{1,2,0:T(8,128)(2,1)S(1)} %copy.44), channel_id=1, source_target_pairs={{1,0},{3,2},{5,4},{7,6},{9,8},{11,10},{13,12},{15,14},{17,16},{19,... | collective-permute-start | bytes 147464 | tf_op jit(solution)/shard_map/ppermute | solution.py:24
  15.7 6.8 %collective-permute-start.2 = (bf16[48,64,8]{1,2,0:T(8,128)(2,1)S(1)}, bf16[48,64,8]{1,2,0:T(8,128)(2,1)S(1)}, u32[]{:S(2)}, u32[]{:S(2)}) collective-permute-start(bf16[48,64,8]{1,2,0:T(8,128)(2,1)S(1)} %copy.43), channel_id=1, source_target_pairs={{0,1},{2,3},{4,5},{6,7},{8,9},{10,11},{12,13},{14,15},{16,17},{18,... | collective-permute-start | bytes 147464 | tf_op jit(solution)/shard_map/ppermute | solution.py:22
  34.4 10.0 %copy-start.12 = (bf16[32,64,256]{2,1,0:T(8,128)(2,1)}, bf16[32,64,256]{2,1,0:T(8,128)(2,1)S(1)}, u32[]{:S(2)}) copy-start(bf16[32,64,256]{2,1,0:T(8,128)(2,1)S(1)} %fusion.1) | copy-start | bytes 3145732
  34.8 7.0 %collective-permute-start.4 = (bf16[8,64,256]{2,1,0:T(8,128)(2,1)S(1)}, bf16[8,64,256]{2,1,0:T(8,128)(2,1)S(1)}, u32[]{:S(2)}, u32[]{:S(2)}) collective-permute-start(bf16[8,64,256]{2,1,0:T(8,128)(2,1)S(1)} %get-tuple-element.52), channel_id=1, source_target_pairs={{0,2},{2,4},{4,6},{6,8},{8,10},{10,12},{12,14},{14,16},{16,18},{18... | collective-permute-start | bytes 786440 | tf_op jit(solution)/shard_map/ppermute | solution.py:22
  40.3 3.9 %collective-permute-start.5 = (bf16[8,64,256]{2,1,0:T(8,128)(2,1)S(1)}, bf16[8,64,256]{2,1,0:T(8,128)(2,1)S(1)}, u32[]{:S(2)}, u32[]{:S(2)}) collective-permute-start(bf16[8,64,256]{2,1,0:T(8,128)(2,1)S(1)} %get-tuple-element.53), channel_id=1, source_target_pairs={{2,0},{4,2},{6,4},{8,6},{10,8},{12,10},{14,12},{16,14},{18,16},{20... | collective-permute-start | bytes 786440 | tf_op jit(solution)/shard_map/ppermute | solution.py:24
  44.4 12.1 %copy-start.35 = (s32[32,256]{1,0:T(8,128)S(1)}, s32[32,256]{1,0:T(8,128)}, u32[]{:S(2)}) copy-start(s32[32,256]{1,0:T(8,128)} %param.16) | copy-start | bytes 98308
  44.4 12.9 %copy-start.27 = (bf16[3,3,64,64]{3,2,1,0:T(8,128)(2,1)S(1)}, bf16[3,3,64,64]{3,2,1,0:T(8,128)(2,1)}, u32[]{:S(2)}) copy-start(bf16[3,3,64,64]{3,2,1,0:T(8,128)(2,1)} %param.12) | copy-start | bytes 221188
  45.8 12.9 %copy-start.28 = (bf16[3,3,64,64]{2,3,1,0:T(8,128)(2,1)S(1)}, bf16[3,3,64,64]{2,3,1,0:T(8,128)(2,1)}, u32[]{:S(2)}) copy-start(bf16[3,3,64,64]{2,3,1,0:T(8,128)(2,1)} %reverse_bitcast_fusion.1) | copy-start | bytes 221188
  48.8 12.1 %collective-permute-start.7 = (bf16[48,64,8]{1,2,0:T(8,128)(2,1)}, bf16[48,64,8]{1,2,0:T(8,128)(2,1)}, u32[]{:S(2)}, u32[]{:S(2)}) collective-permute-start(bf16[48,64,8]{1,2,0:T(8,128)(2,1)} %copy.49), channel_id=1, source_target_pairs={{1,0},{3,2},{5,4},{7,6},{9,8},{11,10},{13,12},{15,14},{17,16},{19,... | collective-permute-start | bytes 147464 | tf_op jit(solution)/shard_map/ppermute | solution.py:24
  50.1 9.6 %collective-permute-start.6 = (bf16[48,64,8]{1,2,0:T(8,128)(2,1)}, bf16[48,64,8]{1,2,0:T(8,128)(2,1)}, u32[]{:S(2)}, u32[]{:S(2)}) collective-permute-start(bf16[48,64,8]{1,2,0:T(8,128)(2,1)} %copy.48), channel_id=1, source_target_pairs={{0,1},{2,3},{4,5},{6,7},{8,9},{10,11},{12,13},{14,15},{16,17},{18,... | collective-permute-start | bytes 147464 | tf_op jit(solution)/shard_map/ppermute | solution.py:22
  73.0 42.2 %copy-start.13 = (bf16[32,64,256]{2,1,0:T(8,128)(2,1)}, bf16[32,64,256]{2,1,0:T(8,128)(2,1)S(1)}, u32[]{:S(2)}) copy-start(bf16[32,64,256]{2,1,0:T(8,128)(2,1)S(1)} %fusion.4) | copy-start | bytes 3145732
  118.8 14.9 %copy-start.14 = (bf16[32,64,256]{2,1,0:T(8,128)(2,1)S(1)}, bf16[32,64,256]{2,1,0:T(8,128)(2,1)}, u32[]{:S(2)}) copy-start(bf16[32,64,256]{2,1,0:T(8,128)(2,1)} %copy-done.13) | copy-start | bytes 3145732
  118.8 14.9 %copy-start.15 = (f32[32,37,256]{2,1,0:T(8,128)S(1)}, f32[32,37,256]{2,1,0:T(8,128)}, u32[]{:S(2)}) copy-start(f32[32,37,256]{2,1,0:T(8,128)} %get-tuple-element.61) | copy-start | bytes 3637252
  118.8 14.9 %copy-start.31 = (f32[32,256]{1,0:T(8,128)S(1)}, f32[32,256]{1,0:T(8,128)}, u32[]{:S(2)}) copy-start(f32[32,256]{1,0:T(8,128)} %get-tuple-element.60) | copy-start | bytes 98308
  118.8 14.9 %copy-start.33 = (s32[32,256]{1,0:T(8,128)S(1)}, s32[32,256]{1,0:T(8,128)}, u32[]{:S(2)}) copy-start(s32[32,256]{1,0:T(8,128)} %reshape.115) | copy-start | bytes 98308
  118.8 14.9 %copy-start.36 = (s32[32,256]{1,0:T(8,128)S(1)}, s32[32,256]{1,0:T(8,128)}, u32[]{:S(2)}) copy-start(s32[32,256]{1,0:T(8,128)} %param.16) | copy-start | bytes 98308
  127.0 9.7 %collective-permute-start.8 = (bf16[8,64,256]{2,1,0:T(8,128)(2,1)}, bf16[8,64,256]{2,1,0:T(8,128)(2,1)}, u32[]{:S(2)}, u32[]{:S(2)}) collective-permute-start(bf16[8,64,256]{2,1,0:T(8,128)(2,1)} %get-tuple-element.46), channel_id=1, source_target_pairs={{0,2},{2,4},{4,6},{6,8},{8,10},{10,12},{12,14},{14,16},{16,18},{18... | collective-permute-start | bytes 786440 | tf_op jit(solution)/shard_map/ppermute | solution.py:22
  132.3 7.0 %collective-permute-start.9 = (bf16[8,64,256]{2,1,0:T(8,128)(2,1)}, bf16[8,64,256]{2,1,0:T(8,128)(2,1)}, u32[]{:S(2)}, u32[]{:S(2)}) collective-permute-start(bf16[8,64,256]{2,1,0:T(8,128)(2,1)} %get-tuple-element.47), channel_id=1, source_target_pairs={{2,0},{4,2},{6,4},{8,6},{10,8},{12,10},{14,12},{16,14},{18,16},{20... | collective-permute-start | bytes 786440 | tf_op jit(solution)/shard_map/ppermute | solution.py:24
  146.1 30.0 %collective-permute-start.11 = (bf16[48,64,8]{1,2,0:T(8,128)(2,1)}, bf16[48,64,8]{1,2,0:T(8,128)(2,1)}, u32[]{:S(2)}, u32[]{:S(2)}) collective-permute-start(bf16[48,64,8]{1,2,0:T(8,128)(2,1)} %copy.61), channel_id=1, source_target_pairs={{1,0},{3,2},{5,4},{7,6},{9,8},{11,10},{13,12},{15,14},{17,16},{19,... | collective-permute-start | bytes 147464 | tf_op jit(solution)/shard_map/ppermute | solution.py:24
  147.4 26.7 %collective-permute-start.10 = (bf16[48,64,8]{1,2,0:T(8,128)(2,1)}, bf16[48,64,8]{1,2,0:T(8,128)(2,1)}, u32[]{:S(2)}, u32[]{:S(2)}) collective-permute-start(bf16[48,64,8]{1,2,0:T(8,128)(2,1)} %copy.60), channel_id=1, source_target_pairs={{0,1},{2,3},{4,5},{6,7},{8,9},{10,11},{12,13},{14,15},{16,17},{18,... | collective-permute-start | bytes 147464 | tf_op jit(solution)/shard_map/ppermute | solution.py:22
  186.8 9.7 %copy-start.16 = (f32[32,37,256]{2,1,0:T(8,128)S(1)}, f32[32,37,256]{2,1,0:T(8,128)}, u32[]{:S(2)}) copy-start(f32[32,37,256]{2,1,0:T(8,128)} %get-tuple-element.61) | copy-start | bytes 3637252
  186.8 9.7 %copy-start.32 = (f32[32,256]{1,0:T(8,128)S(1)}, f32[32,256]{1,0:T(8,128)}, u32[]{:S(2)}) copy-start(f32[32,256]{1,0:T(8,128)} %get-tuple-element.60) | copy-start | bytes 98308
  186.8 9.7 %copy-start.34 = (s32[32,256]{1,0:T(8,128)S(1)}, s32[32,256]{1,0:T(8,128)}, u32[]{:S(2)}) copy-start(s32[32,256]{1,0:T(8,128)} %reshape.115) | copy-start | bytes 98308
  187.7 9.6 %collective-permute-start.12 = (bf16[8,64,256]{2,1,0:T(8,128)(2,1)S(1)}, bf16[8,64,256]{2,1,0:T(8,128)(2,1)S(1)}, u32[]{:S(2)}, u32[]{:S(2)}) collective-permute-start(bf16[8,64,256]{2,1,0:T(8,128)(2,1)S(1)} %get-tuple-element.44), channel_id=1, source_target_pairs={{0,2},{2,4},{4,6},{6,8},{8,10},{10,12},{12,14},{14,16},{16,18},{18... | collective-permute-start | bytes 786440 | tf_op jit(solution)/shard_map/ppermute | solution.py:22
  195.0 11.9 %collective-permute-start.13 = (bf16[8,64,256]{2,1,0:T(8,128)(2,1)S(1)}, bf16[8,64,256]{2,1,0:T(8,128)(2,1)S(1)}, u32[]{:S(2)}, u32[]{:S(2)}) collective-permute-start(bf16[8,64,256]{2,1,0:T(8,128)(2,1)S(1)} %get-tuple-element.45), channel_id=1, source_target_pairs={{2,0},{4,2},{6,4},{8,6},{10,8},{12,10},{14,12},{16,14},{18,16},{20... | collective-permute-start | bytes 786440 | tf_op jit(solution)/shard_map/ppermute | solution.py:24
  197.3 11.4 %copy-start.23 = (bf16[8,64,256]{2,1,0:T(8,128)(2,1)}, bf16[8,64,256]{2,1,0:T(8,128)(2,1)S(1)}, u32[]{:S(2)}) copy-start(bf16[8,64,256]{2,1,0:T(8,128)(2,1)S(1)} %collective-permute-done.12) | copy-start | bytes 786436
  212.8 18.6 %collective-permute-start.15 = (bf16[48,64,8]{1,2,0:T(8,128)(2,1)}, bf16[48,64,8]{1,2,0:T(8,128)(2,1)}, u32[]{:S(2)}, u32[]{:S(2)}) collective-permute-start(bf16[48,64,8]{1,2,0:T(8,128)(2,1)} %copy.67), channel_id=1, source_target_pairs={{1,0},{3,2},{5,4},{7,6},{9,8},{11,10},{13,12},{15,14},{17,16},{19,... | collective-permute-start | bytes 147464 | tf_op jit(solution)/shard_map/ppermute | solution.py:24
  214.0 15.2 %collective-permute-start.14 = (bf16[48,64,8]{1,2,0:T(8,128)(2,1)}, bf16[48,64,8]{1,2,0:T(8,128)(2,1)}, u32[]{:S(2)}, u32[]{:S(2)}) collective-permute-start(bf16[48,64,8]{1,2,0:T(8,128)(2,1)} %copy.66), channel_id=1, source_target_pairs={{0,1},{2,3},{4,5},{6,7},{8,9},{10,11},{12,13},{14,15},{16,17},{18,... | collective-permute-start | bytes 147464 | tf_op jit(solution)/shard_map/ppermute | solution.py:22
  245.3 39.8 %copy-start.1 = (bf16[64,37]{0,1:T(8,128)(2,1)S(1)}, bf16[64,37]{0,1:T(8,128)(2,1)}, u32[]{:S(2)}) copy-start(bf16[64,37]{0,1:T(8,128)(2,1)} %param.14) | copy-start | bytes 14212
  (26 other events, 94.3 us)
